TPU v7x, 256 devices: a whole 4x4x8 slice. The times are simulated.
256 devices in a mesh: site: 32 (over z, x), real: 8 (over y, core).
Axes of the slice: x: 4, y: 4, z: 8, core: 2. Of those that a mesh axis runs over, the one named last changes fastest.
Arguments:
- epsilon: bfloat16 [32768, 4096], P('site', 'real'), may hold values from -6 to 6
- factor: bfloat16 [2, 288, 512, 512], P(None, 'site'), may hold values from -0.09375 to 0.09375
- block_rows: int32 [2, 288], P(None, 'site'), may hold values from 0 to 63, as said below
- median_log: float32 [32768], P('site'), may hold values from -2.5 to -0.5
- spread_log: float32 [32768], P('site'), may hold values from 0.4 to 0.8
- critical_yield: float32 [32768], P('site'), may hold values from 0.03 to 0.3
Outputs:
- residual_field: bfloat16 [32768, 4096], P('site', 'real')
- mean_damage: float32 [32768], P('site')
Inputs may be any that keep to these rules, and one draw needn't show every extreme that they name: block_rows[p, b] = (c + o) mod 64, with c = 2 * (b // 9) + p the block's column tile and o in 0 to 11; the offsets o of one block column are distinct, and the first block of each column has o = 0.
All inputs are finite; a program needn't handle non-finite values.
Results may differ from a plain program's by a relative error of at most 0.001.
Values sent between devices are 32-bit elements; how exact they have to be, the bound alone decides.
No kernel may reach another device: no remote copies, remote signals or barrier semaphores. Data moves between devices by JAX's collectives and lax.ppermute only.
A program may use at most 256 MiB of HBM per device.

v0:
```python
import jax
import jax.numpy as jnp
from jax import lax
from jax.sharding import PartitionSpec as P

BAND = 12


coeff_disp = 10.0**0.215
power_margin = 2.341
power_ratio = 1.438


def passed_along(value, axis, steps):
    count = lax.axis_size(axis)
    pairs = [(source, (source + steps) % count) for source in range(count)]
    return lax.ppermute(value, axis, pairs)


def copy_for_each(x, axis):
    length = lax.axis_size(axis)
    return lax.all_to_all(jnp.broadcast_to(x[None], (length, *x.shape)), axis, 0, 0, tiled=True)


def of_everyone(x, axis):
    everything = copy_for_each(x, axis)
    return jnp.sum(everything, axis=0)


def shards(epsilon, factor, block_rows, median_log, spread_log, critical_yield):
    panels = factor.shape[0]
    per_column = factor.shape[1]
    tile_size = factor.shape[-1]
    own_reals = epsilon.shape[1]
    reach = BAND // 2
    own_index = lax.axis_index("site")
    total_tiles = panels * lax.axis_size("site")
    draws = epsilon.reshape(panels, tile_size, own_reals)

    def pending(panel):
        flat = factor[panel].reshape(per_column * tile_size, tile_size)
        products = jnp.dot(flat, draws[panel], preferred_element_type=jnp.float32)
        products = products.reshape(per_column, tile_size, own_reals)
        relative = ((block_rows[panel] - own_index * panels) % total_tiles).astype(jnp.int32)
        slots = jnp.zeros(((reach + 1) * panels, tile_size, own_reals), jnp.float32)
        sums = slots.at[relative].set(products, unique_indices=True)
        return sums.reshape(reach + 1, panels, tile_size, own_reals)

    def deliver(stack):
        held = {offset: stack[offset] for offset in range(reach + 1)}
        for bit_number in range(reach.bit_length()):
            stride = 1 << bit_number
            moving = [offset for offset in sorted(held) if offset & stride]
            if moving:
                packed = jnp.stack([held[offset] for offset in moving])
                landed = passed_along(packed, "site", stride)
                for place, offset in enumerate(moving):
                    target = offset - stride
                    held.pop(offset)
                    if target in held:
                        held[target] = held[target] + landed[place]
                    else:
                        held[target] = landed[place]
        return held[0]

    combined = pending(0)
    for panel in range(1, panels):
        combined = combined + pending(panel)
    arrived = deliver(combined)
    residual_field = arrived.astype(jnp.bfloat16).reshape(panels * tile_size, own_reals)
    log_peak = median_log[:, None] + spread_log[:, None] * residual_field.astype(jnp.float32)
    log_ratio = jnp.log(critical_yield)[:, None] - log_peak
    ratio = jnp.exp(log_ratio)
    margin = jnp.maximum(1.0 - ratio, 0.0)
    displacement = coeff_disp * jnp.power(margin, power_margin) * jnp.exp(-power_ratio * log_ratio)
    local_total = jnp.sum(jnp.log1p(displacement), axis=1)
    total = of_everyone(local_total, "real")
    mean_damage = total / (own_reals * lax.axis_size("real"))
    return (residual_field, mean_damage)


def solution(mesh):
    return jax.shard_map(
        shards,
        mesh=mesh,
        in_specs=(
            P("site", "real"),
            P(None, "site", None, None),
            P(None, "site"),
            P("site"),
            P("site"),
            P("site"),
        ),
        out_specs=(P("site", "real"), P("site")),
        check_vma=False,
    )
```

profile of v0, /device:TPU:1, one launch (start us, length us, event | category | flops | bytes accessed | tf_op | source)
XLA Modules:
  0.0 394.2 jit_solution(18189460148037147445)
XLA Ops:
  0.6 0.0 copy-start.1
  0.6 0.0 copy-start.3
  0.7 8.8 %fusion.2 = f32[9,512,512]{2,1,0:T(8,128)} fusion(bf16[2,9,512,512]{3,2,1,0:T(8,128)(2,1)} %param.7, bf16[1024,512]{1,0:T(8,128)(2,1)} %param.6), kind=kOutput, calls=%fused_computation.5 | convolution fusion | flops 2415919104 | bytes 14680064 | tf_op jit(solution)/shard_map/dot_general | solution.py:42
  9.4 0.0 copy-done.1
  9.4 0.0 copy-done.3
  9.4 0.0 copy-start.7
  9.5 5.0 %fusion = f32[9,512,512]{2,1,0:T(8,128)} fusion(bf16[2,9,512,512]{3,2,1,0:T(8,128)(2,1)S(1)} %copy-done.1, bf16[1024,512]{1,0:T(8,128)(2,1)S(1)} %copy-done.3), kind=kOutput, calls=%fused_computation.3 | convolution fusion | flops 2415919104 | bytes 14680064 | tf_op jit(solution)/shard_map/dot_general | solution.py:42
  14.5 0.0 copy-done.7
  14.5 7.1 %broadcast.147.clone = f32[14,512,512]{2,1,0:T(8,128)} broadcast(f32[]{:T(128)} %constant.16.clone.1), dimensions={} | broadcast | bytes 14680068 | tf_op jit(solution)/shard_map/broadcast.7
  21.6 18.3 %scatter_fusion = f32[14,512,512]{2,1,0:T(8,128)} fusion(f32[14,512,512]{2,1,0:T(8,128)} %broadcast.147.clone, s32[9]{0:T(128)S(1)} %get-tuple-element.9, f32[9,512,512]{2,1,0:T(8,128)} %fusion.2), kind=kCustom, calls=%fused_computation | custom fusion | bytes 28311588 | tf_op jit(solution)/shard_map/scatter | solution.py:46
  39.9 7.1 %broadcast.147.clone.1 = f32[14,512,512]{2,1,0:T(8,128)} broadcast(f32[]{:T(128)} %constant.16.clone.1), dimensions={} | broadcast | bytes 14680068 | tf_op jit(solution)/shard_map/broadcast.7
  47.0 18.3 %scatter_fusion.1 = f32[14,512,512]{2,1,0:T(8,128)} fusion(f32[14,512,512]{2,1,0:T(8,128)} %broadcast.147.clone.1, s32[9]{0:T(128)S(1)} %get-tuple-element.8, f32[9,512,512]{2,1,0:T(8,128)} %fusion), kind=kCustom, calls=%fused_computation.1 | custom fusion | bytes 28311588 | tf_op jit(solution)/shard_map/scatter | solution.py:46
  65.3 10.6 %add.93 = f32[14,512,512]{2,1,0:T(8,128)S(1)} add(f32[14,512,512]{2,1,0:T(8,128)} %scatter_fusion, f32[14,512,512]{2,1,0:T(8,128)} %scatter_fusion.1) | non-fusion elementwise | flops 3670016 | bytes 44040192 | tf_op jit(solution)/shard_map/add | solution.py:68
  75.9 0.0 copy-start
  75.9 3.1 slice_bitcast_fusion.5
  79.0 3.9 pad_maximum_fusion
  82.9 2.2 collective-permute-start
  85.1 141.9 %collective-permute-done = f32[3,2,512,512]{3,2,1,0:T(8,128)} collective-permute-done((f32[3,2,512,512]{3,2,1,0:T(8,128)S(1)}, f32[3,2,512,512]{3,2,1,0:T(8,128)}, u32[]{:S(2)}, u32[]{:S(2)}) %collective-permute-start) | collective-permute-done | bytes 6291488 | tf_op jit(solution)/shard_map/ppermute | solution.py:17
  227.0 2.1 slice_add_fusion.3
  229.1 0.5 pad_maximum_fusion.1
  229.5 0.0 copy-start.4
  229.6 0.0 copy-start.5
  229.6 0.0 copy-start.6
  229.6 0.1 collective-permute-start.1
  229.7 94.4 %collective-permute-done.1 = f32[2,2,512,512]{3,2,1,0:T(8,128)S(1)} collective-permute-done((f32[2,2,512,512]{3,2,1,0:T(8,128)S(1)}, f32[2,2,512,512]{3,2,1,0:T(8,128)S(1)}, u32[]{:S(2)}, u32[]{:S(2)}) %collective-permute-start.1) | collective-permute-done | bytes 4194336 | tf_op jit(solution)/shard_map/ppermute | solution.py:17
  324.1 0.0 copy-done
  324.1 0.0 copy-start.2
  324.1 5.2 %slice_add_fusion = f32[1,2,512,512]{3,2,1,0:T(8,128)} fusion(f32[2,2,512,512]{3,2,1,0:T(8,128)S(1)} %collective-permute-done.1, f32[3,2,512,512]{3,2,1,0:T(8,128)} %collective-permute-done, f32[14,512,512]{2,1,0:T(8,128)S(1)} %add.93), kind=kLoop, calls=%fused_computation.10 | loop fusion | flops 1048576 | bytes 8388608 | tf_op jit(solution)/shard_map/add | solution.py:61
  329.3 0.0 copy-done.2
  329.3 0.0 collective-permute-start.2
  329.3 0.0 copy-done.4
  329.4 0.0 copy-done.5
  329.4 0.0 copy-done.6
  329.4 46.3 %collective-permute-done.2 = f32[1,2,512,512]{3,2,1,0:T(8,128)S(1)} collective-permute-done((f32[1,2,512,512]{3,2,1,0:T(8,128)}, f32[1,2,512,512]{3,2,1,0:T(8,128)S(1)}, u32[]{:S(2)}, u32[]{:S(2)}) %collective-permute-start.2) | collective-permute-done | bytes 2097184 | tf_op jit(solution)/shard_map/ppermute | solution.py:17
  375.7 5.8 %log-plus-one_reduce_fusion = (f32[2,512]{1,0:T(2,128)S(1)}, bf16[1,2,512,512]{3,2,1,0:T(8,128)(2,1)}) fusion(f32[2,512]{1,0:T(2,128)S(1)} %mul.34, f32[2,512]{1,0:T(2,128)S(1)} %add.100, f32[2,512]{1,0:T(2,128)S(1)} %sub.54, f32[1,2,512,512]{3,2,1,0:T(8,128)S(1)} %collective-permute-done.2, f32[2,2,512,512]{3,2,1,0:T(8,128)} %copy-done.2, ...), kind=kLoop, calls=%fused_computation.24 | loop fusion | flops 7339008 | bytes 9453568 | tf_op jit(solution)/shard_map/reduce_sum | solution.py:76
  381.6 12.0 %all_to_all.6 = f32[8,1,1024]{2,1,0:T(1,128)S(1)} all-to-all(f32[8,1,1024]{2,1,0:T(1,128)S(1)} %broadcast_in_dim.5), channel_id=1, replica_groups=mesh['site'=32,'real'=8] {'real'}, dimensions={0} | all-to-all | bytes 65536 | tf_op jit(solution)/shard_map/all_to_all | solution.py:22
  393.6 0.6 broadcast_multiply_fusion
  (8 shorter events, 0.1 us)
Async XLA Ops:
  0.6 8.8 %copy-start.1 = (bf16[2,9,512,512]{3,2,1,0:T(8,128)(2,1)S(1)}, bf16[2,9,512,512]{3,2,1,0:T(8,128)(2,1)}, u32[]{:S(2)}) copy-start(bf16[2,9,512,512]{3,2,1,0:T(8,128)(2,1)} %param.7) | copy-start | bytes 28311556
  0.6 8.8 %copy-start.3 = (bf16[1024,512]{1,0:T(8,128)(2,1)S(1)}, bf16[1024,512]{1,0:T(8,128)(2,1)}, u32[]{:S(2)}) copy-start(bf16[1024,512]{1,0:T(8,128)(2,1)} %param.6) | copy-start | bytes 3145732
  9.4 5.0 %copy-start.7 = (s32[2,9]{1,0:T(2,128)S(1)}, s32[2,9]{1,0:T(2,128)}, u32[]{:S(2)}) copy-start(s32[2,9]{1,0:T(2,128)} %param.8) | copy-start | bytes 220
  75.9 248.2 %copy-start = (f32[14,512,512]{2,1,0:T(8,128)}, f32[14,512,512]{2,1,0:T(8,128)S(1)}, u32[]{:S(2)}) copy-start(f32[14,512,512]{2,1,0:T(8,128)S(1)} %add.93) | copy-start | bytes 44040196
  82.9 144.1 %collective-permute-start = (f32[3,2,512,512]{3,2,1,0:T(8,128)S(1)}, f32[3,2,512,512]{3,2,1,0:T(8,128)}, u32[]{:S(2)}, u32[]{:S(2)}) collective-permute-start(f32[3,2,512,512]{3,2,1,0:T(8,128)S(1)} %pad_maximum_fusion), channel_id=1, source_target_pairs={{0,8},{8,16},{16,24},{24,32},{32,40},{40,48},{48,56},{56,64},{64,7... | collective-permute-start | bytes 18874376 | tf_op jit(solution)/shard_map/ppermute | solution.py:17
  229.5 99.8 %copy-start.4 = (f32[1024]{0:T(1024)S(1)}, f32[1024]{0:T(1024)}, u32[]{:S(2)}) copy-start(f32[1024]{0:T(1024)} %param.11) | copy-start | bytes 12292
  229.6 99.8 %copy-start.5 = (f32[1024]{0:T(1024)S(1)}, f32[1024]{0:T(1024)}, u32[]{:S(2)}) copy-start(f32[1024]{0:T(1024)} %param.9) | copy-start | bytes 12292
  229.6 99.8 %copy-start.6 = (f32[1024]{0:T(1024)S(1)}, f32[1024]{0:T(1024)}, u32[]{:S(2)}) copy-start(f32[1024]{0:T(1024)} %param.10) | copy-start | bytes 12292
  229.6 94.5 %collective-permute-start.1 = (f32[2,2,512,512]{3,2,1,0:T(8,128)S(1)}, f32[2,2,512,512]{3,2,1,0:T(8,128)S(1)}, u32[]{:S(2)}, u32[]{:S(2)}) collective-permute-start(f32[2,2,512,512]{3,2,1,0:T(8,128)S(1)} %pad_maximum_fusion.1), channel_id=1, source_target_pairs={{0,16},{8,24},{16,32},{24,40},{32,48},{40,56},{48,64},{56,72},{64,... | collective-permute-start | bytes 12582920 | tf_op jit(solution)/shard_map/ppermute | solution.py:17
  324.1 5.2 %copy-start.2 = (f32[2,2,512,512]{3,2,1,0:T(8,128)}, f32[2,2,512,512]{3,2,1,0:T(8,128)S(1)}, u32[]{:S(2)}) copy-start(f32[2,2,512,512]{3,2,1,0:T(8,128)S(1)} %collective-permute-done.1) | copy-start | bytes 12582916
  329.3 46.4 %collective-permute-start.2 = (f32[1,2,512,512]{3,2,1,0:T(8,128)}, f32[1,2,512,512]{3,2,1,0:T(8,128)S(1)}, u32[]{:S(2)}, u32[]{:S(2)}) collective-permute-start(f32[1,2,512,512]{3,2,1,0:T(8,128)} %slice_add_fusion), channel_id=1, source_target_pairs={{0,32},{8,40},{16,48},{24,56},{32,64},{40,72},{48,80},{56,88},{64,... | collective-permute-start | bytes 6291464 | tf_op jit(solution)/shard_map/ppermute | solution.py:17
where the time goes:
time: 395 us; the launch traced here: 394 us
  waiting for transfers between devices  283 us (72%)
  local copies, waits for them, and re-layouts  54 us (14%)
  other arithmetic  28.7 us (7%)
  matrix products  13.8 us (3%)
  blocking collectives  12 us (3%)
    ppermute x3, waiting for transfers between devices, passed_along(): return lax.ppermute(value, axis, pairs)  283 us
    scatter x2, local copies, waits for them, and re-layouts, pending(): sums = slots.at[relative].set(products, unique_indices=True)  36.6 us
    another operation x2, local copies, waits for them, and re-layouts  14.1 us
    dot_general x2, matrix products, pending(): products = jnp.dot(flat, draws[panel], preferred_element_type=jnp.float32)  13.8 us
    all_to_all x1, blocking collectives, copy_for_each(): lax.all_to_all(jnp.broadcast_to(x[None], (length, *x.shape)), axis, 0, 0,...  12 us
    add x1, other arithmetic, shards(): combined = combined + pending(panel)  10.6 us
  transfers between devices with their start and end apart: 3, of which 3 were waited for; matrix products, arithmetic and copies ran while one was open for 0% of the time, Pallas kernels for 0%

commit v1 on v0

v1 whole, which is shorter than its diff:
```python
import jax
import jax.numpy as jnp
from jax import lax
from jax.experimental import pallas as pl
from jax.experimental.pallas import tpu as pltpu
from jax.sharding import PartitionSpec as P

COLUMNS = 4
CHUNKS = ((1, 0, 192), (1, 192, 512), (0, 0, 320), (0, 320, 512))
NONE = 13

coeff_disp = 10.0**0.215
power_margin = 2.341
power_ratio = 1.438

UP = {c: (1, c) for c in range(4)}
RIGHT = {0: (0, 1), 1: (0, 2), 2: (0, 3), 3: (0, 0)}
LEFT = {0: (0, 3), 1: (0, 0), 2: (0, 1), 3: (0, 2)}
CROSS = {0: (0, 2), 1: (0, 3), 2: (0, 0), 3: (0, 1)}
DOWN = {c: (-1, c) for c in range(4)}
MOSTLY_DOWN = {0: (-1, 0), 1: (-1, 1), 2: (-1, 2), 3: (1, 3)}
HALF_DOWN = {0: (-1, 0), 1: (-1, 1), 2: (1, 2), 3: (1, 3)}
TWICE_UP = {0: (2, 0)}


def slot_sums(plan):
    def body(rows_ref, factor_ref, draws_ref, *refs):
        outs = refs[: sum(len(cuts) for _, cuts in plan)]
        table, blocks_ref, sums_ref, draws_vmem, in_sem, draws_sem, out_sem = refs[len(outs) :]
        panels, blocks = factor_ref.shape[:2]
        site = lax.axis_index("site")
        tiles = panels * lax.axis_size("site")
        column = lax.rem(site, COLUMNS)
        load = pltpu.make_async_copy(draws_ref, draws_vmem, draws_sem)
        load.start()
        for p in range(panels):
            for slot in range(NONE + 1):
                table[p, slot] = -1
        for p in range(panels):
            for b in range(blocks):
                table[p, lax.rem(rows_ref[p, b] - panels * site + tiles, tiles)] = b
        found, loads = [], []
        for i, (slot_of, _) in enumerate(plan):
            slot = slot_of(column)
            for p in range(panels):
                b = table[p, slot]
                found.append(b)
                copy = pltpu.make_async_copy(
                    factor_ref.at[p, jnp.maximum(b, 0)], blocks_ref.at[panels * i + p], in_sem.at[panels * i + p]
                )
                copy.start()
                loads.append(copy)
        load.wait()
        stores = []
        for i, (_, cuts) in enumerate(plan):
            for p in range(panels):
                n = panels * i + p
                loads[n].wait()
                b = found[n]

                @pl.when(b >= 0)
                def _():
                    product = jnp.dot(blocks_ref[n], draws_vmem[p], preferred_element_type=jnp.float32)
                    if p == 0:
                        sums_ref[i] = product
                    else:
                        sums_ref[i] += product

                if p == 0:

                    @pl.when(b < 0)
                    def _():
                        sums_ref[i] = jnp.zeros(sums_ref.shape[1:], jnp.float32)

            for low, high in cuts:
                k = len(stores)
                copy = pltpu.make_async_copy(sums_ref.at[i, pl.ds(low, high - low)], outs[k], out_sem.at[k])
                copy.start()
                stores.append(copy)
        for copy in stores:
            copy.wait()

    return body


def sums_of(plan, block_rows, factor, draws):
    panels, blocks, tile, _ = factor.shape
    reals = draws.shape[-1]
    count = len(plan)
    sizes = [high - low for _, cuts in plan for low, high in cuts]
    anywhere = pl.BlockSpec(memory_space=pl.ANY)
    return pl.pallas_call(
        slot_sums(plan),
        in_specs=[pl.BlockSpec(memory_space=pltpu.SMEM), anywhere, anywhere],
        out_specs=[anywhere] * len(sizes),
        out_shape=[jax.ShapeDtypeStruct((n, reals), jnp.float32) for n in sizes],
        scratch_shapes=[
            pltpu.SMEM((2, 16), jnp.int32),
            pltpu.VMEM((panels * count, tile, tile), factor.dtype),
            pltpu.VMEM((count, tile, reals), jnp.float32),
            pltpu.VMEM(draws.shape, draws.dtype),
            pltpu.SemaphoreType.DMA((panels * count,)),
            pltpu.SemaphoreType.DMA,
            pltpu.SemaphoreType.DMA((len(sizes),)),
        ],
        cost_estimate=pl.CostEstimate(
            flops=2 * panels * count * tile * tile * reals,
            bytes_accessed=panels * count * tile * tile * 2 + count * tile * reals * 4,
            transcendentals=0,
        ),
        compiler_params=pltpu.CompilerParams(vmem_limit_bytes=56 << 20),
    )(block_rows, factor, draws)


def after(value, *others):
    return lax.optimization_barrier((value, *others))[0]


def shards(epsilon, factor, block_rows, median_log, spread_log, critical_yield):
    panels = factor.shape[0]
    tile_size = factor.shape[-1]
    own_reals = epsilon.shape[1]
    planes = lax.axis_size("site") // COLUMNS
    column = lax.rem(lax.axis_index("site"), COLUMNS)
    draws = epsilon.reshape(panels, tile_size, own_reals)

    def send(value, moves):
        pairs = []
        for z in range(planes):
            for x, (up, target) in moves.items():
                pairs.append((z * COLUMNS + x, ((z + up) % planes) * COLUMNS + target))
        return lax.ppermute(value, "site", pairs)

    def at(slot):
        return lambda c: slot

    whole = ((0, tile_size),)
    cuts = [tuple((low, high) for t, low, high in CHUNKS if t == tile) for tile in range(panels)]
    first = [
        (at(3), cuts[1]),
        (at(5), whole),
        (lambda c: jnp.where(c < 2, 4, 12), whole),
        (at(7), whole),
    ]
    rest = [
        (at(11), whole),
        (lambda c: jnp.where(c < 3, 2, 10), cuts[0]),
        (lambda c: jnp.where(c < 2, 12, 4), whole),
        (at(6), whole),
        (at(9), whole),
        (lambda c: jnp.where(c < 3, 10, 2), whole),
        (at(8), whole),
        (at(1), whole),
        (at(0), whole),
    ]
    *away1, second1, second0, third1 = sums_of(first, block_rows, factor, draws)
    far1, *away0, kept0, third0, fourth1, far0, fourth0, own1, own0 = sums_of(rest, block_rows, factor, draws)
    aways = {1: away1, 0: away0}
    fars, fourths, owns = {1: far1, 0: far0}, {1: fourth1, 0: fourth0}, {1: own1, 0: own0}

    near = [None] * len(CHUNKS)
    near[0] = send(away1[0], DOWN)
    crossed1 = send(second1, CROSS)
    left1 = send(third1, LEFT)
    vertical = send(second0, HALF_DOWN)
    crossed0 = send(kept0 + vertical, CROSS)
    left0 = send(after(third0, left1), LEFT)
    crossed, lefts = {1: crossed1, 0: crossed0}, {1: left1, 0: left0}

    log_yield = jnp.log(critical_yield)
    fields, totals = {}, {}
    for n, (t, low, high) in enumerate(CHUNKS):
        rows = slice(low, high)
        if n:
            away = aways[t][[c[:2] for c in CHUNKS if c[0] == t].index((t, low))]
            near[n] = send(after(away, crossed1, near[n - 1]), DOWN if t else MOSTLY_DOWN)
        right = send(fars[t][rows] + near[n], RIGHT)
        left, cross = lefts[t][rows], crossed[t][rows]
        onward = fourths[t][rows] + jnp.where(column == 3, 0.0, left)
        field = owns[t][rows] + jnp.where(column == 3, left, 0.0)
        if t:
            onward = onward + jnp.where(column == 0, 0.0, right) + jnp.where(column < 2, cross, 0.0)
            field = field + jnp.where(column < 2, 0.0, cross) + send(right, TWICE_UP)
        else:
            onward = onward + right + cross
        field = (field + send(onward, UP)).astype(jnp.bfloat16)
        here = slice(t * tile_size + low, t * tile_size + high)
        log_peak = median_log[here, None] + spread_log[here, None] * field.astype(jnp.float32)
        log_ratio = log_yield[here, None] - log_peak
        ratio = jnp.exp(log_ratio)
        margin = jnp.maximum(1.0 - ratio, 0.0)
        displacement = coeff_disp * jnp.power(margin, power_margin) * jnp.exp(-power_ratio * log_ratio)
        fields[t, low] = field
        totals[t, low] = jnp.sum(jnp.log1p(displacement), axis=1)
    order = sorted(fields)
    residual_field = jnp.concatenate([fields[k] for k in order], axis=0)
    local_total = jnp.concatenate([totals[k] for k in order], axis=0)
    reals = lax.axis_size("real")
    copies = jnp.broadcast_to(local_total[None], (reals, local_total.shape[0]))
    everything = lax.all_to_all(copies, "real", 0, 0, tiled=True)
    mean_damage = jnp.sum(everything, axis=0) / (own_reals * reals)
    return residual_field, mean_damage


def solution(mesh):
    return jax.shard_map(
        shards,
        mesh=mesh,
        in_specs=(
            P("site", "real"),
            P(None, "site", None, None),
            P(None, "site"),
            P("site"),
            P("site"),
            P("site"),
        ),
        out_specs=(P("site", "real"), P("site")),
        check_vma=False,
    )
```

time: 395 us -> 206 us (0.52)
  waiting for transfers between devices: 283 us -> 136 us
  local copies, waits for them, and re-layouts: 54 us -> 0.97 us
  starting transfers between devices: 2.25 us -> 39.7 us
  other arithmetic: 28.7 us -> 9.22 us
  Pallas kernels: 0 us -> 18.2 us
  matrix products: 13.8 us -> 0 us
  blocking collectives: 12 us -> 0 us
    ppermute x3 -> x19, waiting for transfers between devices: 283 us -> 133 us  [send(): return lax.ppermute(value, 'site', pairs)]
    scatter x2 -> x0, local copies, waits for them, and re-layouts: 36.6 us -> none  [pending(): sums = slots.at[relative].set(products, unique_indices=True)]
    ppermute x3 -> x19, starting transfers between devices: 2.25 us -> 31.8 us  [send(): return lax.ppermute(value, 'site', pairs)]
    pallas_call x0 -> x2, Pallas kernels: none -> 18.2 us  [sums_of(): pl.pallas_call(slot_sums(plan), in_specs=[pl.BlockSpec(memory_space=pltpu...]
    another operation x2 -> x0, local copies, waits for them, and re-layouts: 14.1 us -> none
    add x3 -> x9, other arithmetic: 17.9 us -> 3.93 us  [the longest x1 1.54 us: shards(): crossed0 = send(kept0 + vertical, CROSS)]
    dot_general x2 -> x0, matrix products: 13.8 us -> none  [pending(): products = jnp.dot(flat, draws[panel], preferred_element_type=jnp.float32)]
    all_to_all x1 -> x0, blocking collectives: 12 us -> none  [copy_for_each(): lax.all_to_all(jnp.broadcast_to(x[None], (length, *x.shape)), axis, 0, 0,...]
  transfers between devices with their start and end apart: 3 -> 20, of which waited for: 3 -> 12; matrix products, arithmetic and copies ran while one was open for 0% -> 4% of each run, Pallas kernels for 0% -> 6%
where the time goes in v1:
time: 206 us; the launch traced here: 205 us
  waiting for transfers between devices  136 us (66%)
  starting transfers between devices  39.7 us (19%)
  Pallas kernels  18.2 us (9%)
  other arithmetic  9.22 us (4%)
    ppermute x19, waiting for transfers between devices, send(): return lax.ppermute(value, 'site', pairs)  133 us
    ppermute x19, starting transfers between devices, send(): return lax.ppermute(value, 'site', pairs)  31.8 us
    pallas_call x2, Pallas kernels, sums_of(): pl.pallas_call(slot_sums(plan), in_specs=[pl.BlockSpec(memory_space=pltpu...  18.2 us
    all_to_all x1, starting transfers between devices, shards(): everything = lax.all_to_all(copies, 'real', 0, 0, tiled=True)  7.82 us
  transfers between devices with their start and end apart: 20, of which 12 were waited for; matrix products, arithmetic and copies ran while one was open for 4% of the time, Pallas kernels for 6%

profile of v1, /device:TPU:1, one launch (start us, length us, event | category | flops | bytes accessed | tf_op | source)
XLA Modules:
  0.0 205.3 jit_solution(856545083808555539)
XLA Ops:
  0.6 0.0 copy-start.8
  0.7 6.5 %shard_map.78 = (f32[192,512]{1,0:T(8,128)}, f32[320,512]{1,0:T(8,128)}, f32[512,512]{1,0:T(8,128)}, f32[512,512]{1,0:T(8,128)}, f32[512,512]{1,0:T(8,128)}) custom-call(s32[2,9]{1,0:T(2,128)} %rows_ref.3, bf16[2,9,512,512]{3,2,1,0:T(8,128)(2,1)} %factor_ref.3, bf16[2,512,512]{2,1,0:T(8,128)(2,1)} %bitcast.1), custom_call_target="tpu_custom_call" | custom-call | flops 2147483648 | bytes 8388608 | tf_op jit(solution)/shard_map/pallas_call | solution.py:92
  7.2 4.0 %collective-permute-start.2 = (f32[512,512]{1,0:T(8,128)}, f32[512,512]{1,0:T(8,128)S(1)}, u32[]{:S(2)}, u32[]{:S(2)}) collective-permute-start(f32[512,512]{1,0:T(8,128)} %get-tuple-element.28), channel_id=1, source_target_pairs={{0,16},{8,24},{16,0},{24,8},{32,48},{40,56},{48,32},{56,40},{64,80... | collective-permute-start | bytes 3145736 | tf_op jit(solution)/shard_map/ppermute | solution.py:132
  11.2 5.5 %collective-permute-start.3 = (f32[192,512]{1,0:T(8,128)}, f32[192,512]{1,0:T(8,128)S(1)}, u32[]{:S(2)}, u32[]{:S(2)}) collective-permute-start(f32[192,512]{1,0:T(8,128)} %get-tuple-element.30), channel_id=1, source_target_pairs={{0,224},{8,232},{16,240},{24,248},{32,0},{40,8},{48,16},{56,24},{6... | collective-permute-start | bytes 1179656 | tf_op jit(solution)/shard_map/ppermute | solution.py:132
  16.7 1.3 collective-permute-start
  18.0 0.0 collective-permute-start.7
  18.1 0.1 fusion.3
  18.1 0.1 fusion
  18.2 6.3 %collective-permute-done.3 = f32[192,512]{1,0:T(8,128)S(1)} collective-permute-done((f32[192,512]{1,0:T(8,128)}, f32[192,512]{1,0:T(8,128)S(1)}, u32[]{:S(2)}, u32[]{:S(2)}) %collective-permute-start.3) | collective-permute-done | bytes 393248 | tf_op jit(solution)/shard_map/ppermute | solution.py:132
  24.5 8.9 %collective-permute-done.2 = f32[512,512]{1,0:T(8,128)S(1)} collective-permute-done((f32[512,512]{1,0:T(8,128)}, f32[512,512]{1,0:T(8,128)S(1)}, u32[]{:S(2)}, u32[]{:S(2)}) %collective-permute-start.2) | collective-permute-done | bytes 1048608 | tf_op jit(solution)/shard_map/ppermute | solution.py:132
  33.4 6.2 %collective-permute-start.4 = (f32[320,512]{1,0:T(8,128)}, f32[320,512]{1,0:T(8,128)S(1)}, u32[]{:S(2)}, u32[]{:S(2)}) collective-permute-start(f32[320,512]{1,0:T(8,128)} %get-tuple-element.31), channel_id=1, source_target_pairs={{0,224},{8,232},{16,240},{24,248},{32,0},{40,8},{48,16},{56,24},{6... | collective-permute-start | bytes 1966088 | tf_op jit(solution)/shard_map/ppermute | solution.py:132
  39.6 0.1 fusion.2
  39.7 11.7 %shard_map.77 = (f32[512,512]{1,0:T(8,128)}, f32[320,512]{1,0:T(8,128)}, f32[192,512]{1,0:T(8,128)}, f32[512,512]{1,0:T(8,128)}, f32[512,512]{1,0:T(8,128)}, /*i...) custom-call(s32[2,9]{1,0:T(2,128)} %rows_ref.3, ...), custom_call_target="tpu_custom_call" | custom-call | flops 4831838208 | bytes 18874368 | tf_op jit(solution)/shard_map/pallas_call | solution.py:92
  51.4 9.6 %collective-permute-done.4 = f32[320,512]{1,0:T(8,128)S(1)} collective-permute-done((f32[320,512]{1,0:T(8,128)}, f32[320,512]{1,0:T(8,128)S(1)}, u32[]{:S(2)}, u32[]{:S(2)}) %collective-permute-start.4) | collective-permute-done | bytes 655392 | tf_op jit(solution)/shard_map/ppermute | solution.py:132
  61.0 3.3 %collective-permute-start.5 = (f32[320,512]{1,0:T(8,128)}, f32[320,512]{1,0:T(8,128)S(1)}, u32[]{:S(2)}, u32[]{:S(2)}) collective-permute-start(f32[320,512]{1,0:T(8,128)} %get-tuple-element.32), channel_id=1, source_target_pairs={{0,224},{8,232},{16,240},{24,56},{32,0},{40,8},{48,16},{56,88},{64... | collective-permute-start | bytes 1966088 | tf_op jit(solution)/shard_map/ppermute | solution.py:132
  64.3 0.1 fusion.5
  64.4 1.1 slice_add_fusion.4
  65.5 1.1 collective-permute-start.13
  66.6 0.0 collective-permute-done
  66.6 1.8 collective-permute-start.1
  68.4 0.0 collective-permute-done.7
  68.5 1.5 add.123
  70.0 0.1 collective-permute-start.8
  70.2 0.1 slice_add_fusion.1
  70.3 0.6 collective-permute-start.16
  70.9 5.9 %collective-permute-done.5 = f32[320,512]{1,0:T(8,128)S(1)} collective-permute-done((f32[320,512]{1,0:T(8,128)}, f32[320,512]{1,0:T(8,128)S(1)}, u32[]{:S(2)}, u32[]{:S(2)}) %collective-permute-start.5) | collective-permute-done | bytes 655392 | tf_op jit(solution)/shard_map/ppermute | solution.py:132
  76.8 3.3 %collective-permute-start.10 = (f32[192,512]{1,0:T(8,128)S(1)}, f32[192,512]{1,0:T(8,128)S(1)}, u32[]{:S(2)}, u32[]{:S(2)}) collective-permute-start(f32[192,512]{1,0:T(8,128)S(1)} %copy-done.9), channel_id=1, source_target_pairs={{0,224},{8,232},{16,240},{24,56},{32,0},{40,8},{48,16},{56,88},{64... | collective-permute-start | bytes 1179656 | tf_op jit(solution)/shard_map/ppermute | solution.py:132
  80.1 0.1 slice_add_fusion.2
  80.2 15.6 %collective-permute-done.13 = f32[192,512]{1,0:T(8,128)S(1)} collective-permute-done((f32[192,512]{1,0:T(8,128)S(1)}, f32[192,512]{1,0:T(8,128)S(1)}, u32[]{:S(2)}, u32[]{:S(2)}) %collective-permute-start.13) | collective-permute-done | bytes 393248 | tf_op jit(solution)/shard_map/ppermute | solution.py:132
  95.8 0.0 collective-permute-start.6
  95.8 0.2 select_add_fusion.1
  96.0 0.0 collective-permute-done.10
  96.0 2.1 collective-permute-start.14
  98.1 0.1 slice_add_fusion.5
  98.1 13.8 %collective-permute-done.16 = f32[320,512]{1,0:T(8,128)S(1)} collective-permute-done((f32[320,512]{1,0:T(8,128)S(1)}, f32[320,512]{1,0:T(8,128)S(1)}, u32[]{:S(2)}, u32[]{:S(2)}) %collective-permute-start.16) | collective-permute-done | bytes 655392 | tf_op jit(solution)/shard_map/ppermute | solution.py:132
  112.0 0.0 collective-permute-start.11
  112.0 0.3 select_add_fusion
  112.3 0.0 collective-permute-done.1
  112.3 0.1 collective-permute-start.15
  112.4 0.0 collective-permute-done.8
  112.4 0.1 collective-permute-start.18
  112.5 13.5 %collective-permute-done.6 = f32[320,512]{1,0:T(8,128)S(1)} collective-permute-done((f32[320,512]{1,0:T(8,128)S(1)}, f32[320,512]{1,0:T(8,128)S(1)}, u32[]{:S(2)}, u32[]{:S(2)}) %collective-permute-start.6) | collective-permute-done | bytes 655392 | tf_op jit(solution)/shard_map/ppermute | solution.py:132
  126.0 1.9 collective-permute-start.17
  127.9 0.3 slice_add_fusion
  128.2 6.2 %collective-permute-done.11 = f32[192,512]{1,0:T(8,128)S(1)} collective-permute-done((f32[192,512]{1,0:T(8,128)S(1)}, f32[192,512]{1,0:T(8,128)S(1)}, u32[]{:S(2)}, u32[]{:S(2)}) %collective-permute-start.11) | collective-permute-done | bytes 393248 | tf_op jit(solution)/shard_map/ppermute | solution.py:132
  134.4 0.0 collective-permute-start.9
  134.4 0.2 slice_add_fusion.3
  134.6 0.0 collective-permute-done.14
  134.6 0.3 collective-permute-start.12
  134.9 0.0 collective-permute-done.15
  134.9 0.7 log-plus-one_reduce_fusion.2
  135.7 3.4 %collective-permute-done.18 = f32[320,512]{1,0:T(8,128)S(1)} collective-permute-done((f32[320,512]{1,0:T(8,128)S(1)}, f32[320,512]{1,0:T(8,128)S(1)}, u32[]{:S(2)}, u32[]{:S(2)}) %collective-permute-start.18) | collective-permute-done | bytes 655392 | tf_op jit(solution)/shard_map/ppermute | solution.py:132
  139.1 27.8 %collective-permute-done.17 = f32[320,512]{1,0:T(8,128)S(1)} collective-permute-done((f32[320,512]{1,0:T(8,128)S(1)}, f32[320,512]{1,0:T(8,128)S(1)}, u32[]{:S(2)}, u32[]{:S(2)}) %collective-permute-start.17) | collective-permute-done | bytes 655392 | tf_op jit(solution)/shard_map/ppermute | solution.py:132
  166.8 1.1 log-plus-one_reduce_fusion
  167.9 21.7 %collective-permute-done.12 = f32[192,512]{1,0:T(8,128)S(1)} collective-permute-done((f32[192,512]{1,0:T(8,128)S(1)}, f32[192,512]{1,0:T(8,128)S(1)}, u32[]{:S(2)}, u32[]{:S(2)}) %collective-permute-start.12) | collective-permute-done | bytes 393248 | tf_op jit(solution)/shard_map/ppermute | solution.py:132
  189.6 0.7 log-plus-one_reduce_fusion.3
  190.3 0.0 collective-permute-done.9
  190.3 1.0 log-plus-one_reduce_fusion.1
  191.4 0.1 pad_maximum_fusion.1
  191.4 0.6 broadcast_in_dim.42
  192.1 7.8 %all-to-all-start = ((f32[8,1,1024]{2,1,0:T(1,128)}), f32[8,1,1024]{2,1,0:T(1,128)S(1)}, u32[]{:S(2)}, u32[]{:S(2)}) async-start(f32[8,1,1024]{2,1,0:T(1,128)} %broadcast_in_dim.42), calls=%async_computation | async-start | bytes 65536 | tf_op jit(solution)/shard_map/all_to_all | solution.py:200
  199.9 1.0 pad_maximum_fusion
  200.9 3.7 %all-to-all-done = f32[8,1,1024]{2,1,0:T(1,128)S(1)} async-done(((f32[8,1,1024]{2,1,0:T(1,128)}), f32[8,1,1024]{2,1,0:T(1,128)S(1)}, u32[]{:S(2)}, u32[]{:S(2)}) %all-to-all-start) | async-done | bytes 32800 | tf_op jit(solution)/shard_map/all_to_all | solution.py:200
  204.7 0.6 broadcast_multiply_fusion
  (21 shorter events, 0.1 us)
Async XLA Ops:
  0.6 17.4 %copy-start.8 = (f32[1024]{0:T(1024)S(1)}, f32[1024]{0:T(1024)}, u32[]{:S(2)}) copy-start(f32[1024]{0:T(1024)} %param.11) | copy-start | bytes 12292
  0.6 17.4 %copy-start.7 = (f32[1024]{0:T(1024)S(1)}, f32[1024]{0:T(1024)}, u32[]{:S(2)}) copy-start(f32[1024]{0:T(1024)} %param.9) | copy-start | bytes 12292
  0.7 39.0 %copy-start.6 = (f32[1024]{0:T(1024)S(1)}, f32[1024]{0:T(1024)}, u32[]{:S(2)}) copy-start(f32[1024]{0:T(1024)} %param.10) | copy-start | bytes 12292
  7.2 26.2 %collective-permute-start.2 = (f32[512,512]{1,0:T(8,128)}, f32[512,512]{1,0:T(8,128)S(1)}, u32[]{:S(2)}, u32[]{:S(2)}) collective-permute-start(f32[512,512]{1,0:T(8,128)} %get-tuple-element.28), channel_id=1, source_target_pairs={{0,16},{8,24},{16,0},{24,8},{32,48},{40,56},{48,32},{56,40},{64,80... | collective-permute-start | bytes 3145736 | tf_op jit(solution)/shard_map/ppermute | solution.py:132
  11.2 13.3 %collective-permute-start.3 = (f32[192,512]{1,0:T(8,128)}, f32[192,512]{1,0:T(8,128)S(1)}, u32[]{:S(2)}, u32[]{:S(2)}) collective-permute-start(f32[192,512]{1,0:T(8,128)} %get-tuple-element.30), channel_id=1, source_target_pairs={{0,224},{8,232},{16,240},{24,248},{32,0},{40,8},{48,16},{56,24},{6... | collective-permute-start | bytes 1179656 | tf_op jit(solution)/shard_map/ppermute | solution.py:132
  16.7 49.9 %collective-permute-start = (f32[512,512]{1,0:T(8,128)}, f32[512,512]{1,0:T(8,128)S(1)}, u32[]{:S(2)}, u32[]{:S(2)}) collective-permute-start(f32[512,512]{1,0:T(8,128)} %get-tuple-element.23), channel_id=1, source_target_pairs={{0,24},{8,0},{16,8},{24,16},{32,56},{40,32},{48,40},{56,48},{64,88... | collective-permute-start | bytes 3145736 | tf_op jit(solution)/shard_map/ppermute | solution.py:132
  18.0 50.4 %collective-permute-start.7 = (f32[512,512]{1,0:T(8,128)}, f32[512,512]{1,0:T(8,128)S(1)}, u32[]{:S(2)}, u32[]{:S(2)}) collective-permute-start(f32[512,512]{1,0:T(8,128)} %get-tuple-element.34), channel_id=1, source_target_pairs={{0,224},{8,232},{16,48},{24,56},{32,0},{40,8},{48,80},{56,88},{64,... | collective-permute-start | bytes 3145736 | tf_op jit(solution)/shard_map/ppermute | solution.py:132
  33.4 27.6 %collective-permute-start.4 = (f32[320,512]{1,0:T(8,128)}, f32[320,512]{1,0:T(8,128)S(1)}, u32[]{:S(2)}, u32[]{:S(2)}) collective-permute-start(f32[320,512]{1,0:T(8,128)} %get-tuple-element.31), channel_id=1, source_target_pairs={{0,224},{8,232},{16,240},{24,248},{32,0},{40,8},{48,16},{56,24},{6... | collective-permute-start | bytes 1966088 | tf_op jit(solution)/shard_map/ppermute | solution.py:132
  61.0 15.8 %collective-permute-start.5 = (f32[320,512]{1,0:T(8,128)}, f32[320,512]{1,0:T(8,128)S(1)}, u32[]{:S(2)}, u32[]{:S(2)}) collective-permute-start(f32[320,512]{1,0:T(8,128)} %get-tuple-element.32), channel_id=1, source_target_pairs={{0,224},{8,232},{16,240},{24,56},{32,0},{40,8},{48,16},{56,88},{64... | collective-permute-start | bytes 1966088 | tf_op jit(solution)/shard_map/ppermute | solution.py:132
  64.4 5.8 %copy-start.4 = (f32[512,512]{1,0:T(8,128)S(1)}, f32[512,512]{1,0:T(8,128)}, u32[]{:S(2)}) copy-start(f32[512,512]{1,0:T(8,128)} %get-tuple-element.38) | copy-start | bytes 3145732
  65.5 30.3 %collective-permute-start.13 = (f32[192,512]{1,0:T(8,128)S(1)}, f32[192,512]{1,0:T(8,128)S(1)}, u32[]{:S(2)}, u32[]{:S(2)}) collective-permute-start(f32[192,512]{1,0:T(8,128)S(1)} %slice_add_fusion.4), channel_id=1, source_target_pairs={{0,8},{8,16},{16,24},{24,0},{32,40},{40,48},{48,56},{56,32},{64,72... | collective-permute-start | bytes 1179656 | tf_op jit(solution)/shard_map/ppermute | solution.py:132
  66.6 45.7 %collective-permute-start.1 = (f32[512,512]{1,0:T(8,128)}, f32[512,512]{1,0:T(8,128)S(1)}, u32[]{:S(2)}, u32[]{:S(2)}) collective-permute-start(f32[512,512]{1,0:T(8,128)} %get-tuple-element.24), channel_id=1, source_target_pairs={{0,24},{8,0},{16,8},{24,16},{32,56},{40,32},{48,40},{56,48},{64,88... | collective-permute-start | bytes 3145736 | tf_op jit(solution)/shard_map/ppermute | solution.py:132
  68.5 8.3 %copy-start.9 = (f32[192,512]{1,0:T(8,128)S(1)}, f32[192,512]{1,0:T(8,128)}, u32[]{:S(2)}) copy-start(f32[192,512]{1,0:T(8,128)} %get-tuple-element.36) | copy-start | bytes 1179652
  68.5 11.6 %copy-start.3 = (f32[512,512]{1,0:T(8,128)S(1)}, f32[512,512]{1,0:T(8,128)}, u32[]{:S(2)}) copy-start(f32[512,512]{1,0:T(8,128)} %get-tuple-element.26) | copy-start | bytes 3145732
  70.0 25.8 %copy-start.1 = (f32[512,512]{1,0:T(8,128)S(1)}, f32[512,512]{1,0:T(8,128)}, u32[]{:S(2)}) copy-start(f32[512,512]{1,0:T(8,128)} %get-tuple-element.39) | copy-start | bytes 3145732
  70.0 42.4 %collective-permute-start.8 = (f32[512,512]{1,0:T(8,128)S(1)}, f32[512,512]{1,0:T(8,128)S(1)}, u32[]{:S(2)}, u32[]{:S(2)}) collective-permute-start(f32[512,512]{1,0:T(8,128)S(1)} %add.123), channel_id=1, source_target_pairs={{0,16},{8,24},{16,0},{24,8},{32,48},{40,56},{48,32},{56,40},{64,80... | collective-permute-start | bytes 3145736 | tf_op jit(solution)/shard_map/ppermute | solution.py:132
  70.3 41.7 %collective-permute-start.16 = (f32[320,512]{1,0:T(8,128)S(1)}, f32[320,512]{1,0:T(8,128)S(1)}, u32[]{:S(2)}, u32[]{:S(2)}) collective-permute-start(f32[320,512]{1,0:T(8,128)S(1)} %slice_add_fusion.1), channel_id=1, source_target_pairs={{0,8},{8,16},{16,24},{24,0},{32,40},{40,48},{48,56},{56,32},{64,72... | collective-permute-start | bytes 1966088 | tf_op jit(solution)/shard_map/ppermute | solution.py:132
  76.8 19.2 %collective-permute-start.10 = (f32[192,512]{1,0:T(8,128)S(1)}, f32[192,512]{1,0:T(8,128)S(1)}, u32[]{:S(2)}, u32[]{:S(2)}) collective-permute-start(f32[192,512]{1,0:T(8,128)S(1)} %copy-done.9), channel_id=1, source_target_pairs={{0,224},{8,232},{16,240},{24,56},{32,0},{40,8},{48,16},{56,88},{64... | collective-permute-start | bytes 1179656 | tf_op jit(solution)/shard_map/ppermute | solution.py:132
  95.8 30.2 %collective-permute-start.6 = (f32[320,512]{1,0:T(8,128)S(1)}, f32[320,512]{1,0:T(8,128)S(1)}, u32[]{:S(2)}, u32[]{:S(2)}) collective-permute-start(f32[320,512]{1,0:T(8,128)S(1)} %slice_add_fusion.2), channel_id=1, source_target_pairs={{0,8},{8,16},{16,24},{24,0},{32,40},{40,48},{48,56},{56,32},{64,72... | collective-permute-start | bytes 1966088 | tf_op jit(solution)/shard_map/ppermute | solution.py:132
  96.0 31.9 %copy-start.2 = (f32[512,512]{1,0:T(8,128)S(1)}, f32[512,512]{1,0:T(8,128)}, u32[]{:S(2)}) copy-start(f32[512,512]{1,0:T(8,128)} %get-tuple-element.25) | copy-start | bytes 3145732
  96.0 38.6 %collective-permute-start.14 = (f32[192,512]{1,0:T(8,128)S(1)}, f32[192,512]{1,0:T(8,128)S(1)}, u32[]{:S(2)}, u32[]{:S(2)}) collective-permute-start(f32[192,512]{1,0:T(8,128)S(1)} %collective-permute-done.13), channel_id=1, source_target_pairs={{0,64},{32,96},{64,128},{96,160},{128,192},{160,224},{192,0},{224,... | collective-permute-start | bytes 1179656 | tf_op jit(solution)/shard_map/ppermute | solution.py:132
  112.0 22.5 %collective-permute-start.11 = (f32[192,512]{1,0:T(8,128)S(1)}, f32[192,512]{1,0:T(8,128)S(1)}, u32[]{:S(2)}, u32[]{:S(2)}) collective-permute-start(f32[192,512]{1,0:T(8,128)S(1)} %slice_add_fusion.5), channel_id=1, source_target_pairs={{0,8},{8,16},{16,24},{24,0},{32,40},{40,48},{48,56},{56,32},{64,72... | collective-permute-start | bytes 1179656 | tf_op jit(solution)/shard_map/ppermute | solution.py:132
  112.3 22.6 %collective-permute-start.15 = (f32[192,512]{1,0:T(8,128)S(1)}, f32[192,512]{1,0:T(8,128)S(1)}, u32[]{:S(2)}, u32[]{:S(2)}) collective-permute-start(f32[192,512]{1,0:T(8,128)S(1)} %select_add_fusion.1), channel_id=1, source_target_pairs={{0,32},{8,40},{16,48},{24,56},{32,64},{40,72},{48,80},{56,88},{64,... | collective-permute-start | bytes 1179656 | tf_op jit(solution)/shard_map/ppermute | solution.py:132
  112.4 26.7 %collective-permute-start.18 = (f32[320,512]{1,0:T(8,128)S(1)}, f32[320,512]{1,0:T(8,128)S(1)}, u32[]{:S(2)}, u32[]{:S(2)}) collective-permute-start(f32[320,512]{1,0:T(8,128)S(1)} %select_add_fusion), channel_id=1, source_target_pairs={{0,32},{8,40},{16,48},{24,56},{32,64},{40,72},{48,80},{56,88},{64,... | collective-permute-start | bytes 1966088 | tf_op jit(solution)/shard_map/ppermute | solution.py:132
  126.0 40.8 %collective-permute-start.17 = (f32[320,512]{1,0:T(8,128)S(1)}, f32[320,512]{1,0:T(8,128)S(1)}, u32[]{:S(2)}, u32[]{:S(2)}) collective-permute-start(f32[320,512]{1,0:T(8,128)S(1)} %collective-permute-done.16), channel_id=1, source_target_pairs={{0,64},{32,96},{64,128},{96,160},{128,192},{160,224},{192,0},{224,... | collective-permute-start | bytes 1966088 | tf_op jit(solution)/shard_map/ppermute | solution.py:132
  127.9 7.0 %copy-start.5 = (f32[512,512]{1,0:T(8,128)S(1)}, f32[512,512]{1,0:T(8,128)}, u32[]{:S(2)}) copy-start(f32[512,512]{1,0:T(8,128)} %get-tuple-element.37) | copy-start | bytes 3145732
  134.4 55.9 %collective-permute-start.9 = (f32[320,512]{1,0:T(8,128)S(1)}, f32[320,512]{1,0:T(8,128)S(1)}, u32[]{:S(2)}, u32[]{:S(2)}) collective-permute-start(f32[320,512]{1,0:T(8,128)S(1)} %slice_add_fusion), channel_id=1, source_target_pairs={{0,32},{8,40},{16,48},{24,56},{32,64},{40,72},{48,80},{56,88},{64,... | collective-permute-start | bytes 1966088 | tf_op jit(solution)/shard_map/ppermute | solution.py:132
  134.6 55.0 %collective-permute-start.12 = (f32[192,512]{1,0:T(8,128)S(1)}, f32[192,512]{1,0:T(8,128)S(1)}, u32[]{:S(2)}, u32[]{:S(2)}) collective-permute-start(f32[192,512]{1,0:T(8,128)S(1)} %slice_add_fusion.3), channel_id=1, source_target_pairs={{0,32},{8,40},{16,48},{24,56},{32,64},{40,72},{48,80},{56,88},{64,... | collective-permute-start | bytes 1179656 | tf_op jit(solution)/shard_map/ppermute | solution.py:132
  135.6 54.0 %copy-start = (f32[512,512]{1,0:T(8,128)S(1)}, f32[512,512]{1,0:T(8,128)}, u32[]{:S(2)}) copy-start(f32[512,512]{1,0:T(8,128)} %get-tuple-element.21) | copy-start | bytes 3145732
  192.1 12.5 %all-to-all-start = ((f32[8,1,1024]{2,1,0:T(1,128)}), f32[8,1,1024]{2,1,0:T(1,128)S(1)}, u32[]{:S(2)}, u32[]{:S(2)}) async-start(f32[8,1,1024]{2,1,0:T(1,128)} %broadcast_in_dim.42), calls=%async_computation | async-start | bytes 65536 | tf_op jit(solution)/shard_map/all_to_all | solution.py:200

commit v2 on v1

v2 whole, which is shorter than its diff:
```python
import jax
import jax.numpy as jnp
from jax import lax
from jax.experimental import pallas as pl
from jax.experimental.pallas import tpu as pltpu
from jax.sharding import PartitionSpec as P

COLUMNS = 4
PIECES = ((0, 256), (256, 512))
NONE = 13

coeff_disp = 10.0**0.215
power_margin = 2.341
power_ratio = 1.438

UP = {c: (1, c) for c in range(4)}
RIGHT = {0: (0, 1), 1: (0, 2), 2: (0, 3), 3: (0, 0)}
LEFT = {0: (0, 3), 1: (0, 0), 2: (0, 1), 3: (0, 2)}
CROSS = {0: (0, 2), 1: (0, 3), 2: (0, 0), 3: (0, 1)}
MOSTLY_DOWN = {0: (-1, 0), 1: (-1, 1), 2: (-1, 2), 3: (1, 3)}
HALF_DOWN = {0: (-1, 0), 1: (-1, 1), 2: (1, 2), 3: (1, 3)}


def slot_sums(plan):
    def body(rows_ref, factor_ref, draws_ref, *refs):
        outs = refs[: sum(len(cuts) for _, cuts in plan)]
        table, blocks_ref, sums_ref, draws_vmem, in_sem, draws_sem, out_sem = refs[len(outs) :]
        panels, blocks, side = factor_ref.shape[:3]
        site = lax.axis_index("site")
        tiles = panels * lax.axis_size("site")
        column = lax.rem(site, COLUMNS)
        load = pltpu.make_async_copy(draws_ref, draws_vmem, draws_sem)
        load.start()
        for p in range(panels):
            for slot in range(NONE + 1):
                table[p, slot] = -1
        for p in range(panels):
            for b in range(blocks):
                table[p, lax.rem(rows_ref[p, b] - panels * site + tiles, tiles)] = b
        found, loads = [], []
        for i, (slot_of, _) in enumerate(plan):
            slot = slot_of(column)
            for p in range(panels):
                b = table[p, slot]
                found.append(b)
                copy = pltpu.make_async_copy(
                    factor_ref.at[p, jnp.maximum(b, 0)],
                    blocks_ref.at[i, :, pl.ds(p * side, side)],
                    in_sem.at[panels * i + p],
                )
                copy.start()
                loads.append(copy)
        load.wait()
        stores = []
        for i, (_, cuts) in enumerate(plan):
            for p in range(panels):
                n = panels * i + p
                loads[n].wait()

                @pl.when(found[n] < 0)
                def _():
                    blocks_ref[i, :, pl.ds(p * side, side)] = jnp.zeros((side, side), blocks_ref.dtype)

            sums_ref[i] = jnp.dot(blocks_ref[i], draws_vmem[...], preferred_element_type=jnp.float32)
            for low, high in cuts:
                k = len(stores)
                copy = pltpu.make_async_copy(sums_ref.at[i, pl.ds(low, high - low)], outs[k], out_sem.at[k])
                copy.start()
                stores.append(copy)
        for copy in stores:
            copy.wait()

    return body


def sums_of(plan, block_rows, factor, draws, cost):
    panels, blocks, tile, _ = factor.shape
    reals = draws.shape[-1]
    count = len(plan)
    sizes = [high - low for _, cuts in plan for low, high in cuts]
    anywhere = pl.BlockSpec(memory_space=pl.ANY)
    return pl.pallas_call(
        slot_sums(plan),
        in_specs=[pl.BlockSpec(memory_space=pltpu.SMEM), anywhere, anywhere],
        out_specs=[anywhere] * len(sizes),
        out_shape=[jax.ShapeDtypeStruct((n, reals), jnp.float32) for n in sizes],
        scratch_shapes=[
            pltpu.SMEM((2, 16), jnp.int32),
            pltpu.VMEM((count, tile, panels * tile), factor.dtype),
            pltpu.VMEM((count, tile, reals), jnp.float32),
            pltpu.VMEM(draws.shape, draws.dtype),
            pltpu.SemaphoreType.DMA((panels * count,)),
            pltpu.SemaphoreType.DMA,
            pltpu.SemaphoreType.DMA((len(sizes),)),
        ],
        cost_estimate=pl.CostEstimate(flops=cost, bytes_accessed=cost, transcendentals=0),
        compiler_params=pltpu.CompilerParams(vmem_limit_bytes=56 << 20),
    )(block_rows, factor, draws)


def after(value, *others):
    return lax.optimization_barrier((value, *others))[0]


def shards(epsilon, factor, block_rows, median_log, spread_log, critical_yield):
    panels = factor.shape[0]
    tile_size = factor.shape[-1]
    own_reals = epsilon.shape[1]
    planes = lax.axis_size("site") // COLUMNS
    column = lax.rem(lax.axis_index("site"), COLUMNS)

    def send(value, moves):
        pairs = []
        for z in range(planes):
            for x, (up, target) in moves.items():
                pairs.append((z * COLUMNS + x, ((z + up) % planes) * COLUMNS + target))
        return lax.ppermute(value, "site", pairs)

    def at(slot):
        return lambda c: slot

    whole = ((0, tile_size),)
    first = [(at(5), whole), (lambda c: jnp.where(c < 3, 3, 11), whole)]
    second = [(at(7), whole), (lambda c: jnp.where(c < 2, 4, 12), whole)]
    third = [(lambda c: jnp.where(c < 3, 11, 3), whole), (lambda c: jnp.where(c < 3, 2, 10), whole), (lambda c: jnp.where(c < 2, 12, 4), whole)]
    rest = [
        (at(6), PIECES),
        (at(9), whole),
        (lambda c: jnp.where(c < 3, 10, 2), whole),
        (at(8), whole),
        (at(1), whole),
        (at(0), whole),
    ]
    second1, away1 = sums_of(first, block_rows, factor, epsilon, 1 << 20)
    third1, second0 = sums_of(second, after(block_rows, second1), factor, epsilon, 1 << 10)
    far1, away0, kept0 = sums_of(third, after(block_rows, second0), factor, epsilon, 1 << 10)

    last = column == 3
    low = column < 2
    cross1 = send(second1, CROSS)
    near1 = send(away1, MOSTLY_DOWN)
    left1 = send(after(third1, cross1), LEFT)
    vertical = send(second0, HALF_DOWN)
    right1 = send(after(far1, cross1) + near1, RIGHT)
    *third0, fourth1, far0, fourth0, own1, own0 = sums_of(rest, after(block_rows, near1), factor, epsilon, 1 << 10)
    middle0 = after(kept0, own0) + vertical
    cross0 = send(middle0, CROSS)
    near0 = send(after(away0, right1, middle0), MOSTLY_DOWN)
    onward1 = fourth1 + right1 + jnp.where(last, 0.0, left1) + jnp.where(low, cross1, 0.0)
    up1 = send(onward1, UP)
    own1 = own1 + jnp.where(low, 0.0, cross1)
    results = [(1, 0, tile_size, own1, up1, left1)]
    before, ready = left1, onward1
    for (start, end), third in zip(PIECES, third0):
        rows = slice(start, end)
        left0 = send(after(third, before), LEFT)
        right0 = send(far0[rows] + near0[rows], RIGHT)
        onward0 = after(fourth0, ready)[rows] + right0 + cross0[rows] + jnp.where(last, 0.0, left0)
        results.append((0, start, end, own0[rows], send(onward0, UP), left0))
        before, ready = left0, onward0

    log_yield = jnp.log(critical_yield)
    fields, totals = {}, {}
    done = log_yield
    for t, start, end, own, up, left in results:
        field = (after(own, done) + up + jnp.where(last, left, 0.0)).astype(jnp.bfloat16)
        here = slice(t * tile_size + start, t * tile_size + end)
        log_peak = median_log[here, None] + spread_log[here, None] * field.astype(jnp.float32)
        log_ratio = log_yield[here, None] - log_peak
        ratio = jnp.exp(log_ratio)
        margin = jnp.maximum(1.0 - ratio, 0.0)
        displacement = coeff_disp * jnp.power(margin, power_margin) * jnp.exp(-power_ratio * log_ratio)
        fields[t, start] = field
        done = totals[t, start] = jnp.sum(jnp.log1p(displacement), axis=1)
    order = sorted(fields)
    residual_field = jnp.concatenate([fields[k] for k in order], axis=0)
    local_total = jnp.concatenate([totals[k] for k in order], axis=0)
    reals = lax.axis_size("real")
    copies = jnp.broadcast_to(local_total[None], (reals, local_total.shape[0]))
    everything = lax.all_to_all(copies, "real", 0, 0, tiled=True)
    mean_damage = jnp.sum(everything, axis=0) / (own_reals * reals)
    return residual_field, mean_damage


def solution(mesh):
    return jax.shard_map(
        shards,
        mesh=mesh,
        in_specs=(
            P("site", "real"),
            P(None, "site", None, None),
            P(None, "site"),
            P("site"),
            P("site"),
            P("site"),
        ),
        out_specs=(P("site", "real"), P("site")),
        check_vma=False,
    )
```

time: 206 us -> 150 us (0.73)
  waiting for transfers between devices: 136 us -> 75.9 us
  Pallas kernels: 18.2 us -> 24.8 us
  starting transfers between devices: 39.7 us -> 33.6 us
    ppermute x19 -> x14, waiting for transfers between devices: 133 us -> 72.2 us  [send(): return lax.ppermute(value, 'site', pairs)]
    ppermute x19 -> x14, starting transfers between devices: 31.8 us -> 23.4 us  [send(): return lax.ppermute(value, 'site', pairs)]
    pallas_call x2 -> x4, Pallas kernels: 18.2 us -> 24.8 us  [sums_of(): pl.pallas_call(slot_sums(plan), in_specs=[pl.BlockSpec(memory_space=pltpu...]
    all_to_all x1, starting transfers between devices: 7.82 us -> 10.1 us  [shards(): everything = lax.all_to_all(copies, 'real', 0, 0, tiled=True)]
    add x9 -> x6, other arithmetic: 3.93 us -> 5.49 us  [the longest x1 1.98 us: shards(): fourth1 + right1 + jnp.where(last, 0.0, left1) + jnp.where(low, cross1, 0.0)]
  transfers between devices with their start and end apart: 20 -> 15, of which waited for: 12 -> 11; matrix products, arithmetic and copies ran while one was open for 4% -> 6% of each run, Pallas kernels for 6% -> 13%
where the time goes in v2:
time: 150 us; the launch traced here: 148 us
  waiting for transfers between devices  75.9 us (51%)
  starting transfers between devices  33.6 us (22%)
  Pallas kernels  24.8 us (17%)
  other arithmetic  10.4 us (7%)
  local copies, waits for them, and re-layouts  2.75 us (2%)
    ppermute x14, waiting for transfers between devices, send(): return lax.ppermute(value, 'site', pairs)  72.2 us
    pallas_call x4, Pallas kernels, sums_of(): pl.pallas_call(slot_sums(plan), in_specs=[pl.BlockSpec(memory_space=pltpu...  24.8 us
    ppermute x14, starting transfers between devices, send(): return lax.ppermute(value, 'site', pairs)  23.4 us
    all_to_all x1, starting transfers between devices, shards(): everything = lax.all_to_all(copies, 'real', 0, 0, tiled=True)  10.1 us
    all_to_all x1, waiting for transfers between devices, shards(): everything = lax.all_to_all(copies, 'real', 0, 0, tiled=True)  3.68 us
    reduce_sum x3, other arithmetic, shards(): done = totals[t, start] = jnp.sum(jnp.log1p(displacement), axis=1)  3.25 us
  transfers between devices with their start and end apart: 15, of which 11 were waited for; matrix products, arithmetic and copies ran while one was open for 6% of the time, Pallas kernels for 13%

profile of v2, /device:TPU:1, one launch (start us, length us, event | category | flops | bytes accessed | tf_op | source)
XLA Modules:
  0.0 148.3 jit_solution(15994403453104112035)
XLA Ops:
  0.6 4.8 %shard_map.77 = (f32[512,512]{1,0:T(8,128)}, f32[512,512]{1,0:T(8,128)}) custom-call(s32[2,9]{1,0:T(2,128)} %rows_ref.4, bf16[2,9,512,512]{3,2,1,0:T(8,128)(2,1)} %factor_ref.7, bf16[1024,512]{1,0:T(8,128)(2,1)} %draws_ref.7), custom_call_target="tpu_custom_call" | custom-call | flops 1048576 | bytes 1048576 | tf_op jit(solution)/shard_map/pallas_call | solution.py:82
  5.4 3.7 %collective-permute-start.1 = (f32[512,512]{1,0:T(8,128)}, f32[512,512]{1,0:T(8,128)S(1)}, u32[]{:S(2)}, u32[]{:S(2)}) collective-permute-start(f32[512,512]{1,0:T(8,128)} %get-tuple-element.34), channel_id=1, source_target_pairs={{0,16},{8,24},{16,0},{24,8},{32,48},{40,56},{48,32},{56,40},{64,80... | collective-permute-start | bytes 3145736 | tf_op jit(solution)/shard_map/ppermute | solution.py:117
  9.1 5.6 %collective-permute-start = (f32[512,512]{1,0:T(8,128)}, f32[512,512]{1,0:T(8,128)S(1)}, u32[]{:S(2)}, u32[]{:S(2)}) collective-permute-start(f32[512,512]{1,0:T(8,128)} %get-tuple-element.30), channel_id=1, source_target_pairs={{0,224},{8,232},{16,240},{24,56},{32,0},{40,8},{48,16},{56,88},{64... | collective-permute-start | bytes 3145736 | tf_op jit(solution)/shard_map/ppermute | solution.py:117
  14.7 4.8 %shard_map.79 = (f32[512,512]{1,0:T(8,128)}, f32[512,512]{1,0:T(8,128)}) custom-call(s32[2,9]{1,0:T(2,128)} %rows_ref.4, bf16[2,9,512,512]{3,2,1,0:T(8,128)(2,1)} %factor_ref.7, bf16[1024,512]{1,0:T(8,128)(2,1)} %draws_ref.7), custom_call_target="tpu_custom_call" | custom-call | flops 1024 | bytes 1024 | tf_op jit(solution)/shard_map/pallas_call | solution.py:82
  19.5 0.8 collective-permute-start.5
  20.3 6.0 %shard_map.80 = (f32[512,512]{1,0:T(8,128)}, f32[512,512]{1,0:T(8,128)}, f32[512,512]{1,0:T(8,128)}) custom-call(s32[2,9]{1,0:T(2,128)} %rows_ref.4, bf16[2,9,512,512]{3,2,1,0:T(8,128)(2,1)} %factor_ref.7, bf16[1024,512]{1,0:T(8,128)(2,1)} %draws_ref.7), custom_call_target="tpu_custom_call" | custom-call | flops 1024 | bytes 1024 | tf_op jit(solution)/shard_map/pallas_call | solution.py:82
  26.4 4.9 %collective-permute-done.1 = f32[512,512]{1,0:T(8,128)S(1)} collective-permute-done((f32[512,512]{1,0:T(8,128)}, f32[512,512]{1,0:T(8,128)S(1)}, u32[]{:S(2)}, u32[]{:S(2)}) %collective-permute-start.1) | collective-permute-done | bytes 1048608 | tf_op jit(solution)/shard_map/ppermute | solution.py:117
  31.3 1.0 copy-done.4
  32.3 4.3 %collective-permute-done = f32[512,512]{1,0:T(8,128)S(1)} collective-permute-done((f32[512,512]{1,0:T(8,128)}, f32[512,512]{1,0:T(8,128)S(1)}, u32[]{:S(2)}, u32[]{:S(2)}) %collective-permute-start) | collective-permute-done | bytes 1048608 | tf_op jit(solution)/shard_map/ppermute | solution.py:117
  36.5 1.4 add.86
  38.0 0.3 collective-permute-start.2
  38.3 2.4 %collective-permute-start.3 = (f32[512,512]{1,0:T(8,128)}, f32[512,512]{1,0:T(8,128)S(1)}, u32[]{:S(2)}, u32[]{:S(2)}) collective-permute-start(f32[512,512]{1,0:T(8,128)} %get-tuple-element.43), channel_id=1, source_target_pairs={{0,24},{8,0},{16,8},{24,16},{32,56},{40,32},{48,40},{56,48},{64,88... | collective-permute-start | bytes 3145736 | tf_op jit(solution)/shard_map/ppermute | solution.py:117
  40.7 9.1 %shard_map.78 = (f32[256,512]{1,0:T(8,128)}, f32[256,512]{1,0:T(8,128)}, f32[512,512]{1,0:T(8,128)}, f32[512,512]{1,0:T(8,128)}, f32[512,512]{1,0:T(8,128)}, /*index=5*/f32[512,512]{1,0:T(8,128)}, f32[512,512]{1,0:T(8,128)}) custom-call(s32[2,9]{1,0:T(2,128)} %rows_ref.4, bf16[2,9,512,512]{3,2,1,0:T(8,128)(2,1)} %factor_ref.7, bf16[1024,512]{1,0:T(8,128)(2,1)} %draws_ref.7), custom_call_target="tpu_custom_call" | custom-call | flops 1024 | bytes 1024 | tf_op jit(solution)/shard_map/pallas_call | solution.py:82
  49.8 0.0 copy-start.9
  49.8 0.0 copy-start.11
  49.8 0.0 copy-start.10
  49.9 0.0 copy-start
  49.9 9.1 %collective-permute-done.5 = f32[512,512]{1,0:T(8,128)S(1)} collective-permute-done((f32[512,512]{1,0:T(8,128)}, f32[512,512]{1,0:T(8,128)S(1)}, u32[]{:S(2)}, u32[]{:S(2)}) %collective-permute-start.5) | collective-permute-done | bytes 1048608 | tf_op jit(solution)/shard_map/ppermute | solution.py:117
  59.0 0.0 copy-done.1
  59.0 0.2 add.93
  59.2 1.4 collective-permute-done.2
  60.6 1.0 copy-done.6
  61.6 3.3 %collective-permute-start.6 = (f32[512,512]{1,0:T(8,128)}, f32[512,512]{1,0:T(8,128)}, u32[]{:S(2)}, u32[]{:S(2)}) collective-permute-start(f32[512,512]{1,0:T(8,128)} %get-tuple-element.51), channel_id=1, source_target_pairs={{0,224},{8,232},{16,240},{24,56},{32,0},{40,8},{48,16},{56,88},{64... | collective-permute-start | bytes 3145736 | tf_op jit(solution)/shard_map/ppermute | solution.py:117
  64.9 0.0 copy-done.9
  64.9 0.0 copy-done.11
  64.9 0.0 copy-done.10
  65.0 1.8 %collective-permute-start.8 = (f32[512,512]{1,0:T(8,128)S(1)}, f32[512,512]{1,0:T(8,128)S(1)}, u32[]{:S(2)}, u32[]{:S(2)}) collective-permute-start(f32[512,512]{1,0:T(8,128)S(1)} %add.93), channel_id=1, source_target_pairs={{0,16},{8,24},{16,0},{24,8},{32,48},{40,56},{48,32},{56,40},{64,80... | collective-permute-start | bytes 3145736 | tf_op jit(solution)/shard_map/ppermute | solution.py:117
  66.8 0.0 collective-permute-done.3
  66.8 0.0 collective-permute-start.9
  66.8 16.6 %collective-permute-done.6 = f32[512,512]{1,0:T(8,128)} collective-permute-done((f32[512,512]{1,0:T(8,128)}, f32[512,512]{1,0:T(8,128)}, u32[]{:S(2)}, u32[]{:S(2)}) %collective-permute-start.6) | collective-permute-done | bytes 1048608 | tf_op jit(solution)/shard_map/ppermute | solution.py:117
  83.4 0.0 copy-done
  83.4 1.4 slice_add_fusion.1
  84.8 0.1 collective-permute-start.7
  84.9 0.0 copy-done.5
  84.9 0.0 copy-done.7
  84.9 0.0 copy-done.8
  84.9 0.0 copy-start.12
  84.9 0.0 copy-start.2
  84.9 2.0 %select_add_fusion = (f32[512,512]{1,0:T(8,128)S(1)}, f32[512,512]{1,0:T(8,128)S(1)}) fusion(f32[512,512]{1,0:T(8,128)S(1)} %copy-done.5, f32[512,512]{1,0:T(8,128)S(1)} %collective-permute-done.3, f32[512,512]{1,0:T(8,128)S(1)} %copy-done.8, f32[512,512]{1,0:T(8,128)S(1)} %copy-done.7, pred[]{:T(512)S(6)} %eq.3, pred[]{:T(512)S(6)} %lt.3, ...), kind=kLoop, calls=%fused_computation.3 | loop fusion | flops 1835008 | bytes 7340034 | tf_op jit(solution)/shard_map/add | solution.py:149
  86.9 0.0 copy-start.3
  86.9 0.1 collective-permute-start.4
  87.0 11.1 %collective-permute-done.9 = f32[256,512]{1,0:T(8,128)S(1)} collective-permute-done((f32[256,512]{1,0:T(8,128)}, f32[256,512]{1,0:T(8,128)S(1)}, u32[]{:S(2)}, u32[]{:S(2)}) %collective-permute-start.9) | collective-permute-done | bytes 524320 | tf_op jit(solution)/shard_map/ppermute | solution.py:117
  98.2 3.3 %collective-permute-start.12 = (f32[256,512]{1,0:T(8,128)S(1)}, f32[256,512]{1,0:T(8,128)S(1)}, u32[]{:S(2)}, u32[]{:S(2)}) collective-permute-start(f32[256,512]{1,0:T(8,128)S(1)} %copy-done.12), channel_id=1, source_target_pairs={{0,24},{8,0},{16,8},{24,16},{32,56},{40,32},{48,40},{56,48},{64,88... | collective-permute-start | bytes 1572872 | tf_op jit(solution)/shard_map/ppermute | solution.py:117
  101.5 0.6 collective-permute-start.11
  102.1 0.1 fusion.2
  102.1 0.0 collective-permute-done.8
  102.2 0.0 collective-permute-done.7
  102.2 0.2 fusion.1
  102.4 0.5 collective-permute-start.10
  102.9 11.0 %collective-permute-done.12 = f32[256,512]{1,0:T(8,128)S(1)} collective-permute-done((f32[256,512]{1,0:T(8,128)S(1)}, f32[256,512]{1,0:T(8,128)S(1)}, u32[]{:S(2)}, u32[]{:S(2)}) %collective-permute-start.12) | collective-permute-done | bytes 524320 | tf_op jit(solution)/shard_map/ppermute | solution.py:117
  113.9 1.5 collective-permute-done.11
  115.4 0.2 fusion
  115.6 1.0 collective-permute-start.13
  116.6 0.0 collective-permute-done.4
  116.6 1.6 %log-plus-one_reduce_fusion = (f32[512]{0:T(512)S(1)}, bf16[512,512]{1,0:T(8,128)(2,1)S(1)}) fusion(f32[512]{0:T(512)S(1)} %slice.60, f32[512]{0:T(512)S(1)} %slice.59, f32[512]{0:T(512)S(1)} %slice.58, f32[512,512]{1,0:T(8,128)S(1)} %collective-permute-done.3, pred[]{:T(512)S(6)} %eq.3, f32[512,512]{1,0:T(8,128)S(1)} %get-tuple-element.35, ...), kind=kLoop, calls=%fused_computation.1 | loop fusion | flops 3669504 | bytes 3678209 | tf_op jit(solution)/shard_map/reduce_sum | solution.py:174
  118.2 1.7 %collective-permute-done.10 = f32[256,512]{1,0:T(8,128)S(1)} collective-permute-done((f32[256,512]{1,0:T(8,128)S(1)}, f32[256,512]{1,0:T(8,128)S(1)}, u32[]{:S(2)}, u32[]{:S(2)}) %collective-permute-start.10) | collective-permute-done | bytes 524320 | tf_op jit(solution)/shard_map/ppermute | solution.py:117
  120.0 0.8 log-plus-one_reduce_fusion.2
  120.8 10.5 %collective-permute-done.13 = f32[256,512]{1,0:T(8,128)S(1)} collective-permute-done((f32[256,512]{1,0:T(8,128)S(1)}, f32[256,512]{1,0:T(8,128)S(1)}, u32[]{:S(2)}, u32[]{:S(2)}) %collective-permute-start.13) | collective-permute-done | bytes 524320 | tf_op jit(solution)/shard_map/ppermute | solution.py:117
  131.3 0.8 log-plus-one_reduce_fusion.1
  132.2 0.6 broadcast_in_dim.20
  132.8 10.1 %all-to-all-start = ((f32[8,1,1024]{2,1,0:T(1,128)}), f32[8,1,1024]{2,1,0:T(1,128)S(1)}, u32[]{:S(2)}, u32[]{:S(2)}) async-start(f32[8,1,1024]{2,1,0:T(1,128)} %broadcast_in_dim.20), calls=%async_computation | async-start | bytes 65536 | tf_op jit(solution)/shard_map/all_to_all | solution.py:180
  143.0 1.0 pad_maximum_fusion
  144.0 3.7 %all-to-all-done = f32[8,1,1024]{2,1,0:T(1,128)S(1)} async-done(((f32[8,1,1024]{2,1,0:T(1,128)}), f32[8,1,1024]{2,1,0:T(1,128)S(1)}, u32[]{:S(2)}, u32[]{:S(2)}) %all-to-all-start) | async-done | bytes 32800 | tf_op jit(solution)/shard_map/all_to_all | solution.py:180
  147.7 0.6 broadcast_multiply_fusion
  (17 shorter events, 0.1 us)
Async XLA Ops:
  5.4 25.8 %collective-permute-start.1 = (f32[512,512]{1,0:T(8,128)}, f32[512,512]{1,0:T(8,128)S(1)}, u32[]{:S(2)}, u32[]{:S(2)}) collective-permute-start(f32[512,512]{1,0:T(8,128)} %get-tuple-element.34), channel_id=1, source_target_pairs={{0,16},{8,24},{16,0},{24,8},{32,48},{40,56},{48,32},{56,40},{64,80... | collective-permute-start | bytes 3145736 | tf_op jit(solution)/shard_map/ppermute | solution.py:117
  9.1 27.4 %collective-permute-start = (f32[512,512]{1,0:T(8,128)}, f32[512,512]{1,0:T(8,128)S(1)}, u32[]{:S(2)}, u32[]{:S(2)}) collective-permute-start(f32[512,512]{1,0:T(8,128)} %get-tuple-element.30), channel_id=1, source_target_pairs={{0,224},{8,232},{16,240},{24,56},{32,0},{40,8},{48,16},{56,88},{64... | collective-permute-start | bytes 3145736 | tf_op jit(solution)/shard_map/ppermute | solution.py:117
  19.5 39.5 %collective-permute-start.5 = (f32[512,512]{1,0:T(8,128)}, f32[512,512]{1,0:T(8,128)S(1)}, u32[]{:S(2)}, u32[]{:S(2)}) collective-permute-start(f32[512,512]{1,0:T(8,128)} %get-tuple-element.38), channel_id=1, source_target_pairs={{0,224},{8,232},{16,48},{24,56},{32,0},{40,8},{48,80},{56,88},{64,... | collective-permute-start | bytes 3145736 | tf_op jit(solution)/shard_map/ppermute | solution.py:117
  31.3 1.0 copy-start.4
  38.0 22.6 %collective-permute-start.2 = (f32[512,512]{1,0:T(8,128)S(1)}, f32[512,512]{1,0:T(8,128)S(1)}, u32[]{:S(2)}, u32[]{:S(2)}) collective-permute-start(f32[512,512]{1,0:T(8,128)S(1)} %add.86), channel_id=1, source_target_pairs={{0,8},{8,16},{16,24},{24,0},{32,40},{40,48},{48,56},{56,32},{64,72... | collective-permute-start | bytes 3145736 | tf_op jit(solution)/shard_map/ppermute | solution.py:117
  38.3 20.7 %copy-start.1 = (f32[512,512]{1,0:T(8,128)S(1)}, f32[512,512]{1,0:T(8,128)}, u32[]{:S(2)}) copy-start(f32[512,512]{1,0:T(8,128)} %get-tuple-element.50) | copy-start | bytes 3145732
  38.3 28.5 %collective-permute-start.3 = (f32[512,512]{1,0:T(8,128)}, f32[512,512]{1,0:T(8,128)S(1)}, u32[]{:S(2)}, u32[]{:S(2)}) collective-permute-start(f32[512,512]{1,0:T(8,128)} %get-tuple-element.43), channel_id=1, source_target_pairs={{0,24},{8,0},{16,8},{24,16},{32,56},{40,32},{48,40},{56,48},{64,88... | collective-permute-start | bytes 3145736 | tf_op jit(solution)/shard_map/ppermute | solution.py:117
  49.8 15.0 %copy-start.9 = (f32[1024]{0:T(1024)S(1)}, f32[1024]{0:T(1024)}, u32[]{:S(2)}) copy-start(f32[1024]{0:T(1024)} %param.11) | copy-start | bytes 12292
  49.8 15.1 %copy-start.11 = (f32[1024]{0:T(1024)S(1)}, f32[1024]{0:T(1024)}, u32[]{:S(2)}) copy-start(f32[1024]{0:T(1024)} %param.9) | copy-start | bytes 12292
  49.8 15.1 %copy-start.10 = (f32[1024]{0:T(1024)S(1)}, f32[1024]{0:T(1024)}, u32[]{:S(2)}) copy-start(f32[1024]{0:T(1024)} %param.10) | copy-start | bytes 12292
  49.9 33.5 %copy-start = (f32[512,512]{1,0:T(8,128)S(1)}, f32[512,512]{1,0:T(8,128)}, u32[]{:S(2)}) copy-start(f32[512,512]{1,0:T(8,128)} %get-tuple-element.47) | copy-start | bytes 3145732
  60.6 1.0 copy-start.6
  61.6 21.8 %collective-permute-start.6 = (f32[512,512]{1,0:T(8,128)}, f32[512,512]{1,0:T(8,128)}, u32[]{:S(2)}, u32[]{:S(2)}) collective-permute-start(f32[512,512]{1,0:T(8,128)} %get-tuple-element.51), channel_id=1, source_target_pairs={{0,224},{8,232},{16,240},{24,56},{32,0},{40,8},{48,16},{56,88},{64... | collective-permute-start | bytes 3145736 | tf_op jit(solution)/shard_map/ppermute | solution.py:117
  64.9 20.0 %copy-start.5 = (f32[512,512]{1,0:T(8,128)S(1)}, f32[512,512]{1,0:T(8,128)}, u32[]{:S(2)}) copy-start(f32[512,512]{1,0:T(8,128)} %copy-done.4) | copy-start | bytes 3145732
  64.9 20.0 %copy-start.7 = (f32[512,512]{1,0:T(8,128)S(1)}, f32[512,512]{1,0:T(8,128)}, u32[]{:S(2)}) copy-start(f32[512,512]{1,0:T(8,128)} %copy-done.6) | copy-start | bytes 3145732
  64.9 20.0 %copy-start.8 = (f32[512,512]{1,0:T(8,128)S(1)}, f32[512,512]{1,0:T(8,128)}, u32[]{:S(2)}) copy-start(f32[512,512]{1,0:T(8,128)} %get-tuple-element.36) | copy-start | bytes 3145732
  65.0 37.2 %collective-permute-start.8 = (f32[512,512]{1,0:T(8,128)S(1)}, f32[512,512]{1,0:T(8,128)S(1)}, u32[]{:S(2)}, u32[]{:S(2)}) collective-permute-start(f32[512,512]{1,0:T(8,128)S(1)} %add.93), channel_id=1, source_target_pairs={{0,16},{8,24},{16,0},{24,8},{32,48},{40,56},{48,32},{56,40},{64,80... | collective-permute-start | bytes 3145736 | tf_op jit(solution)/shard_map/ppermute | solution.py:117
  66.8 31.4 %collective-permute-start.9 = (f32[256,512]{1,0:T(8,128)}, f32[256,512]{1,0:T(8,128)S(1)}, u32[]{:S(2)}, u32[]{:S(2)}) collective-permute-start(f32[256,512]{1,0:T(8,128)} %get-tuple-element.53), channel_id=1, source_target_pairs={{0,24},{8,0},{16,8},{24,16},{32,56},{40,32},{48,40},{56,48},{64,88... | collective-permute-start | bytes 1572872 | tf_op jit(solution)/shard_map/ppermute | solution.py:117
  84.8 17.4 %collective-permute-start.7 = (f32[256,512]{1,0:T(8,128)S(1)}, f32[256,512]{1,0:T(8,128)S(1)}, u32[]{:S(2)}, u32[]{:S(2)}) collective-permute-start(f32[256,512]{1,0:T(8,128)S(1)} %get-tuple-element.65), channel_id=1, source_target_pairs={{0,8},{8,16},{16,24},{24,0},{32,40},{40,48},{48,56},{56,32},{64,72... | collective-permute-start | bytes 1572872 | tf_op jit(solution)/shard_map/ppermute | solution.py:117
  84.9 13.3 %copy-start.12 = (f32[256,512]{1,0:T(8,128)S(1)}, f32[256,512]{1,0:T(8,128)}, u32[]{:S(2)}) copy-start(f32[256,512]{1,0:T(8,128)} %get-tuple-element.57) | copy-start | bytes 1572868
  84.9 17.1 %copy-start.2 = (f32[512,512]{1,0:T(8,128)S(1)}, f32[512,512]{1,0:T(8,128)}, u32[]{:S(2)}) copy-start(f32[512,512]{1,0:T(8,128)} %get-tuple-element.32) | copy-start | bytes 3145732
  86.9 15.2 %copy-start.3 = (f32[512,512]{1,0:T(8,128)S(1)}, f32[512,512]{1,0:T(8,128)}, u32[]{:S(2)}) copy-start(f32[512,512]{1,0:T(8,128)} %get-tuple-element.55) | copy-start | bytes 3145732
  86.9 29.7 %collective-permute-start.4 = (f32[512,512]{1,0:T(8,128)S(1)}, f32[512,512]{1,0:T(8,128)S(1)}, u32[]{:S(2)}, u32[]{:S(2)}) collective-permute-start(f32[512,512]{1,0:T(8,128)S(1)} %get-tuple-element.68), channel_id=1, source_target_pairs={{0,32},{8,40},{16,48},{24,56},{32,64},{40,72},{48,80},{56,88},{64,... | collective-permute-start | bytes 3145736 | tf_op jit(solution)/shard_map/ppermute | solution.py:117
  98.2 15.7 %collective-permute-start.12 = (f32[256,512]{1,0:T(8,128)S(1)}, f32[256,512]{1,0:T(8,128)S(1)}, u32[]{:S(2)}, u32[]{:S(2)}) collective-permute-start(f32[256,512]{1,0:T(8,128)S(1)} %copy-done.12), channel_id=1, source_target_pairs={{0,24},{8,0},{16,8},{24,16},{32,56},{40,32},{48,40},{56,48},{64,88... | collective-permute-start | bytes 1572872 | tf_op jit(solution)/shard_map/ppermute | solution.py:117
  101.5 13.9 %collective-permute-start.11 = (f32[256,512]{1,0:T(8,128)S(1)}, f32[256,512]{1,0:T(8,128)S(1)}, u32[]{:S(2)}, u32[]{:S(2)}) collective-permute-start(f32[256,512]{1,0:T(8,128)S(1)} %get-tuple-element.64), channel_id=1, source_target_pairs={{0,8},{8,16},{16,24},{24,0},{32,40},{40,48},{48,56},{56,32},{64,72... | collective-permute-start | bytes 1572872 | tf_op jit(solution)/shard_map/ppermute | solution.py:117
  102.4 17.6 %collective-permute-start.10 = (f32[256,512]{1,0:T(8,128)S(1)}, f32[256,512]{1,0:T(8,128)S(1)}, u32[]{:S(2)}, u32[]{:S(2)}) collective-permute-start(f32[256,512]{1,0:T(8,128)S(1)} %fusion.1), channel_id=1, source_target_pairs={{0,32},{8,40},{16,48},{24,56},{32,64},{40,72},{48,80},{56,88},{64,... | collective-permute-start | bytes 1572872 | tf_op jit(solution)/shard_map/ppermute | solution.py:117
  115.6 15.7 %collective-permute-start.13 = (f32[256,512]{1,0:T(8,128)S(1)}, f32[256,512]{1,0:T(8,128)S(1)}, u32[]{:S(2)}, u32[]{:S(2)}) collective-permute-start(f32[256,512]{1,0:T(8,128)S(1)} %fusion), channel_id=1, source_target_pairs={{0,32},{8,40},{16,48},{24,56},{32,64},{40,72},{48,80},{56,88},{64,... | collective-permute-start | bytes 1572872 | tf_op jit(solution)/shard_map/ppermute | solution.py:117
  132.8 14.9 %all-to-all-start = ((f32[8,1,1024]{2,1,0:T(1,128)}), f32[8,1,1024]{2,1,0:T(1,128)S(1)}, u32[]{:S(2)}, u32[]{:S(2)}) async-start(f32[8,1,1024]{2,1,0:T(1,128)} %broadcast_in_dim.20), calls=%async_computation | async-start | bytes 65536 | tf_op jit(solution)/shard_map/all_to_all | solution.py:180

commit v3 on v2

--- a/solution.py
+++ b/solution.py
@@ -150,14 +150,14 @@
     up1 = send(onward1, UP)
     own1 = own1 + jnp.where(low, 0.0, cross1)
     results = [(1, 0, tile_size, own1, up1, left1)]
-    before, ready = left1, onward1
+    before, ready = (left1,), onward1
     for (start, end), third in zip(PIECES, third0):
         rows = slice(start, end)
-        left0 = send(after(third, before), LEFT)
+        left0 = send(after(third, *before), LEFT)
         right0 = send(far0[rows] + near0[rows], RIGHT)
         onward0 = after(fourth0, ready)[rows] + right0 + cross0[rows] + jnp.where(last, 0.0, left0)
         results.append((0, start, end, own0[rows], send(onward0, UP), left0))
-        before, ready = left0, onward0
+        before, ready = (left0, right0), onward0
 
     log_yield = jnp.log(critical_yield)
     fields, totals = {}, {}
@@ -176,9 +176,10 @@
     residual_field = jnp.concatenate([fields[k] for k in order], axis=0)
     local_total = jnp.concatenate([totals[k] for k in order], axis=0)
     reals = lax.axis_size("real")
-    copies = jnp.broadcast_to(local_total[None], (reals, local_total.shape[0]))
-    everything = lax.all_to_all(copies, "real", 0, 0, tiled=True)
-    mean_damage = jnp.sum(everything, axis=0) / (own_reals * reals)
+    pair = local_total + lax.ppermute(local_total, "real", [(i, i ^ 1) for i in range(reals)])
+    around = [lax.ppermute(pair, "real", [(i, (i + 2 * k) % reals) for i in range(reals)]) for k in (1, 2, 3)]
+    everything = (pair + around[1]) + (around[0] + around[2])
+    mean_damage = everything / (own_reals * reals)
     return residual_field, mean_damage
 
 

time: 150 us -> 149 us (level)
  waiting for transfers between devices: 75.9 us -> 73.1 us
    ppermute x0 -> x4, starting transfers between devices: none -> 11.5 us  [the longest x1 5.91 us: shards(): lax.ppermute(local_total, 'real', [(i, i ^ 1) for i in range(reals)])]
    all_to_all x1 -> x0, starting transfers between devices: 10.1 us -> none  [shards(): everything = lax.all_to_all(copies, 'real', 0, 0, tiled=True)]
    all_to_all x1 -> x0, waiting for transfers between devices: 3.68 us -> none  [shards(): everything = lax.all_to_all(copies, 'real', 0, 0, tiled=True)]
  transfers between devices with their start and end apart: 15 -> 18, of which waited for: 11 -> 11; matrix products, arithmetic and copies ran while one was open for 6% -> 6% of each run, Pallas kernels for 13% -> 14%
where the time goes in v3:
time: 149 us; the launch traced here: 146 us
  waiting for transfers between devices  73.1 us (49%)
  starting transfers between devices  34.7 us (23%)
  Pallas kernels  24.8 us (17%)
  other arithmetic  10.4 us (7%)
  local copies, waits for them, and re-layouts  2.13 us (1%)
    ppermute x14, waiting for transfers between devices, send(): return lax.ppermute(value, 'site', pairs)  72.3 us
    pallas_call x4, Pallas kernels, sums_of(): pl.pallas_call(slot_sums(plan), in_specs=[pl.BlockSpec(memory_space=pltpu...  24.8 us
    ppermute x14, starting transfers between devices, send(): return lax.ppermute(value, 'site', pairs)  23.1 us
    ppermute x1, starting transfers between devices, shards(): lax.ppermute(local_total, 'real', [(i, i ^ 1) for i in range(reals)])  5.91 us
    ppermute x3, starting transfers between devices, shards(): lax.ppermute(pair, 'real', [(i, (i + 2 * k) % reals) for i in range(reals)])  5.62 us
    reduce_sum x3, other arithmetic, shards(): done = totals[t, start] = jnp.sum(jnp.log1p(displacement), axis=1)  3.27 us
  transfers between devices with their start and end apart: 18, of which 11 were waited for; matrix products, arithmetic and copies ran while one was open for 6% of the time, Pallas kernels for 14%

profile of v3, /device:TPU:1, one launch (start us, length us, event | category | flops | bytes accessed | tf_op | source)
XLA Modules:
  0.0 146.0 jit_solution(7608664252470072645)
XLA Ops:
  0.6 4.8 %shard_map.77 = (f32[512,512]{1,0:T(8,128)}, f32[512,512]{1,0:T(8,128)}) custom-call(s32[2,9]{1,0:T(2,128)} %rows_ref.4, bf16[2,9,512,512]{3,2,1,0:T(8,128)(2,1)} %factor_ref.7, bf16[1024,512]{1,0:T(8,128)(2,1)} %draws_ref.7), custom_call_target="tpu_custom_call" | custom-call | flops 1048576 | bytes 1048576 | tf_op jit(solution)/shard_map/pallas_call | solution.py:82
  5.4 3.7 %collective-permute-start.1 = (f32[512,512]{1,0:T(8,128)}, f32[512,512]{1,0:T(8,128)S(1)}, u32[]{:S(2)}, u32[]{:S(2)}) collective-permute-start(f32[512,512]{1,0:T(8,128)} %get-tuple-element.34), channel_id=1, source_target_pairs={{0,16},{8,24},{16,0},{24,8},{32,48},{40,56},{48,32},{56,40},{64,80... | collective-permute-start | bytes 3145736 | tf_op jit(solution)/shard_map/ppermute | solution.py:117
  9.1 5.6 %collective-permute-start = (f32[512,512]{1,0:T(8,128)}, f32[512,512]{1,0:T(8,128)S(1)}, u32[]{:S(2)}, u32[]{:S(2)}) collective-permute-start(f32[512,512]{1,0:T(8,128)} %get-tuple-element.30), channel_id=1, source_target_pairs={{0,224},{8,232},{16,240},{24,56},{32,0},{40,8},{48,16},{56,88},{64... | collective-permute-start | bytes 3145736 | tf_op jit(solution)/shard_map/ppermute | solution.py:117
  14.7 4.8 %shard_map.79 = (f32[512,512]{1,0:T(8,128)}, f32[512,512]{1,0:T(8,128)}) custom-call(s32[2,9]{1,0:T(2,128)} %rows_ref.4, bf16[2,9,512,512]{3,2,1,0:T(8,128)(2,1)} %factor_ref.7, bf16[1024,512]{1,0:T(8,128)(2,1)} %draws_ref.7), custom_call_target="tpu_custom_call" | custom-call | flops 1024 | bytes 1024 | tf_op jit(solution)/shard_map/pallas_call | solution.py:82
  19.5 0.8 collective-permute-start.5
  20.3 6.0 %shard_map.80 = (f32[512,512]{1,0:T(8,128)}, f32[512,512]{1,0:T(8,128)}, f32[512,512]{1,0:T(8,128)}) custom-call(s32[2,9]{1,0:T(2,128)} %rows_ref.4, bf16[2,9,512,512]{3,2,1,0:T(8,128)(2,1)} %factor_ref.7, bf16[1024,512]{1,0:T(8,128)(2,1)} %draws_ref.7), custom_call_target="tpu_custom_call" | custom-call | flops 1024 | bytes 1024 | tf_op jit(solution)/shard_map/pallas_call | solution.py:82
  26.3 4.9 %collective-permute-done.1 = f32[512,512]{1,0:T(8,128)S(1)} collective-permute-done((f32[512,512]{1,0:T(8,128)}, f32[512,512]{1,0:T(8,128)S(1)}, u32[]{:S(2)}, u32[]{:S(2)}) %collective-permute-start.1) | collective-permute-done | bytes 1048608 | tf_op jit(solution)/shard_map/ppermute | solution.py:117
  31.3 1.0 copy-done.4
  32.2 4.3 %collective-permute-done = f32[512,512]{1,0:T(8,128)S(1)} collective-permute-done((f32[512,512]{1,0:T(8,128)}, f32[512,512]{1,0:T(8,128)S(1)}, u32[]{:S(2)}, u32[]{:S(2)}) %collective-permute-start) | collective-permute-done | bytes 1048608 | tf_op jit(solution)/shard_map/ppermute | solution.py:117
  36.5 1.4 add.98
  37.9 0.4 collective-permute-start.2
  38.3 2.4 %collective-permute-start.3 = (f32[512,512]{1,0:T(8,128)}, f32[512,512]{1,0:T(8,128)S(1)}, u32[]{:S(2)}, u32[]{:S(2)}) collective-permute-start(f32[512,512]{1,0:T(8,128)} %get-tuple-element.43), channel_id=1, source_target_pairs={{0,24},{8,0},{16,8},{24,16},{32,56},{40,32},{48,40},{56,48},{64,88... | collective-permute-start | bytes 3145736 | tf_op jit(solution)/shard_map/ppermute | solution.py:117
  40.7 9.2 %shard_map.78 = (f32[256,512]{1,0:T(8,128)}, f32[256,512]{1,0:T(8,128)}, f32[512,512]{1,0:T(8,128)}, f32[512,512]{1,0:T(8,128)}, f32[512,512]{1,0:T(8,128)}, /*index=5*/f32[512,512]{1,0:T(8,128)}, f32[512,512]{1,0:T(8,128)}) custom-call(s32[2,9]{1,0:T(2,128)} %rows_ref.4, bf16[2,9,512,512]{3,2,1,0:T(8,128)(2,1)} %factor_ref.7, bf16[1024,512]{1,0:T(8,128)(2,1)} %draws_ref.7), custom_call_target="tpu_custom_call" | custom-call | flops 1024 | bytes 1024 | tf_op jit(solution)/shard_map/pallas_call | solution.py:82
  49.9 0.0 copy-start.9
  49.9 0.0 copy-start.11
  49.9 0.0 copy-start.10
  49.9 9.1 %collective-permute-done.5 = f32[512,512]{1,0:T(8,128)S(1)} collective-permute-done((f32[512,512]{1,0:T(8,128)}, f32[512,512]{1,0:T(8,128)S(1)}, u32[]{:S(2)}, u32[]{:S(2)}) %collective-permute-start.5) | collective-permute-done | bytes 1048608 | tf_op jit(solution)/shard_map/ppermute | solution.py:117
  59.0 0.2 add.105
  59.2 1.3 collective-permute-done.2
  60.6 1.0 copy-done.6
  61.6 3.3 %collective-permute-start.6 = (f32[512,512]{1,0:T(8,128)}, f32[512,512]{1,0:T(8,128)}, u32[]{:S(2)}, u32[]{:S(2)}) collective-permute-start(f32[512,512]{1,0:T(8,128)} %get-tuple-element.51), channel_id=1, source_target_pairs={{0,224},{8,232},{16,240},{24,56},{32,0},{40,8},{48,16},{56,88},{64... | collective-permute-start | bytes 3145736 | tf_op jit(solution)/shard_map/ppermute | solution.py:117
  64.9 0.0 copy-done.11
  64.9 0.0 copy-done.10
  64.9 1.8 %collective-permute-start.8 = (f32[512,512]{1,0:T(8,128)S(1)}, f32[512,512]{1,0:T(8,128)S(1)}, u32[]{:S(2)}, u32[]{:S(2)}) collective-permute-start(f32[512,512]{1,0:T(8,128)S(1)} %add.105), channel_id=1, source_target_pairs={{0,16},{8,24},{16,0},{24,8},{32,48},{40,56},{48,32},{56,40},{64,80... | collective-permute-start | bytes 3145736 | tf_op jit(solution)/shard_map/ppermute | solution.py:117
  66.7 0.0 collective-permute-done.3
  66.7 0.0 collective-permute-start.9
  66.7 16.6 %collective-permute-done.6 = f32[512,512]{1,0:T(8,128)} collective-permute-done((f32[512,512]{1,0:T(8,128)}, f32[512,512]{1,0:T(8,128)}, u32[]{:S(2)}, u32[]{:S(2)}) %collective-permute-start.6) | collective-permute-done | bytes 1048608 | tf_op jit(solution)/shard_map/ppermute | solution.py:117
  83.4 1.4 slice_add_fusion.1
  84.8 0.1 collective-permute-start.7
  84.9 0.0 copy-done.5
  84.9 0.0 copy-done.7
  84.9 0.0 copy-done.8
  84.9 0.0 copy-start.12
  84.9 0.0 copy-start.2
  84.9 2.0 %select_add_fusion = (f32[512,512]{1,0:T(8,128)S(1)}, f32[512,512]{1,0:T(8,128)S(1)}) fusion(f32[512,512]{1,0:T(8,128)S(1)} %copy-done.5, f32[512,512]{1,0:T(8,128)S(1)} %collective-permute-done.3, f32[512,512]{1,0:T(8,128)S(1)} %copy-done.8, f32[512,512]{1,0:T(8,128)S(1)} %copy-done.7, pred[]{:T(512)S(6)} %eq.3, pred[]{:T(512)S(6)} %lt.3, ...), kind=kLoop, calls=%fused_computation.3 | loop fusion | flops 1835008 | bytes 7340034 | tf_op jit(solution)/shard_map/add | solution.py:149
  86.9 0.1 collective-permute-start.4
  87.0 2.7 %collective-permute-start.11 = (f32[256,512]{1,0:T(8,128)S(1)}, f32[256,512]{1,0:T(8,128)S(1)}, u32[]{:S(2)}, u32[]{:S(2)}) collective-permute-start(f32[256,512]{1,0:T(8,128)S(1)} %get-tuple-element.64), channel_id=1, source_target_pairs={{0,8},{8,16},{16,24},{24,0},{32,40},{40,48},{48,56},{56,32},{64,72... | collective-permute-start | bytes 1572872 | tf_op jit(solution)/shard_map/ppermute | solution.py:117
  89.7 8.4 %collective-permute-done.9 = f32[256,512]{1,0:T(8,128)S(1)} collective-permute-done((f32[256,512]{1,0:T(8,128)}, f32[256,512]{1,0:T(8,128)S(1)}, u32[]{:S(2)}, u32[]{:S(2)}) %collective-permute-start.9) | collective-permute-done | bytes 524320 | tf_op jit(solution)/shard_map/ppermute | solution.py:117
  98.1 2.1 %collective-permute-done.7 = f32[256,512]{1,0:T(8,128)S(1)} collective-permute-done((f32[256,512]{1,0:T(8,128)S(1)}, f32[256,512]{1,0:T(8,128)S(1)}, u32[]{:S(2)}, u32[]{:S(2)}) %collective-permute-start.7) | collective-permute-done | bytes 524320 | tf_op jit(solution)/shard_map/ppermute | solution.py:117
  100.2 1.2 collective-permute-start.12
  101.4 0.1 fusion.3
  101.5 0.0 collective-permute-done.8
  101.5 0.2 fusion.1
  101.8 1.1 collective-permute-start.10
  102.9 8.5 %collective-permute-done.11 = f32[256,512]{1,0:T(8,128)S(1)} collective-permute-done((f32[256,512]{1,0:T(8,128)S(1)}, f32[256,512]{1,0:T(8,128)S(1)}, u32[]{:S(2)}, u32[]{:S(2)}) %collective-permute-start.11) | collective-permute-done | bytes 524320 | tf_op jit(solution)/shard_map/ppermute | solution.py:117
  111.4 0.0 collective-permute-done.12
  111.4 0.2 fusion
  111.7 0.1 collective-permute-start.13
  111.7 0.0 collective-permute-done.4
  111.8 1.6 %log-plus-one_reduce_fusion = (f32[512]{0:T(512)S(1)}, bf16[512,512]{1,0:T(8,128)(2,1)S(1)}) fusion(f32[512]{0:T(512)S(1)} %slice.60, f32[512]{0:T(512)S(1)} %slice.59, f32[512]{0:T(512)S(1)} %slice.58, f32[512,512]{1,0:T(8,128)S(1)} %collective-permute-done.3, pred[]{:T(512)S(6)} %eq.3, f32[512,512]{1,0:T(8,128)S(1)} %get-tuple-element.35, ...), kind=kLoop, calls=%fused_computation.1 | loop fusion | flops 3669504 | bytes 3678209 | tf_op jit(solution)/shard_map/reduce_sum | solution.py:174
  113.3 6.6 %collective-permute-done.10 = f32[256,512]{1,0:T(8,128)S(1)} collective-permute-done((f32[256,512]{1,0:T(8,128)S(1)}, f32[256,512]{1,0:T(8,128)S(1)}, u32[]{:S(2)}, u32[]{:S(2)}) %collective-permute-start.10) | collective-permute-done | bytes 524320 | tf_op jit(solution)/shard_map/ppermute | solution.py:117
  119.9 0.8 log-plus-one_reduce_fusion.2
  120.8 10.4 %collective-permute-done.13 = f32[256,512]{1,0:T(8,128)S(1)} collective-permute-done((f32[256,512]{1,0:T(8,128)S(1)}, f32[256,512]{1,0:T(8,128)S(1)}, u32[]{:S(2)}, u32[]{:S(2)}) %collective-permute-start.13) | collective-permute-done | bytes 524320 | tf_op jit(solution)/shard_map/ppermute | solution.py:117
  131.2 0.8 log-plus-one_reduce_fusion.1
  132.0 5.9 %collective-permute-start.14 = (f32[1024]{0:T(1024)S(1)}, f32[1024]{0:T(1024)S(1)}, u32[]{:S(2)}, u32[]{:S(2)}) collective-permute-start(f32[1024]{0:T(1024)S(1)} %pad_maximum_fusion.1), channel_id=1, source_target_pairs={{0,1},{1,0},{2,3},{3,2},{4,5},{5,4},{6,7},{7,6},{8,9},{9,8},{10,11... | collective-permute-start | bytes 12296 | tf_op jit(solution)/shard_map/ppermute | solution.py:179
  137.9 0.8 collective-permute-done.14
  138.8 2.9 %collective-permute-start.15 = (f32[1024]{0:T(1024)S(1)}, f32[1024]{0:T(1024)S(1)}, u32[]{:S(2)}, u32[]{:S(2)}) collective-permute-start(f32[1024]{0:T(1024)S(1)} %fusion.2), channel_id=1, source_target_pairs={{0,4},{1,5},{2,6},{3,7},{4,0},{5,1},{6,2},{7,3},{8,12},{9,13},{10,... | collective-permute-start | bytes 12296 | tf_op jit(solution)/shard_map/ppermute | solution.py:180
  141.7 0.4 collective-permute-start.16
  142.1 2.3 %collective-permute-start.17 = (f32[1024]{0:T(1024)S(1)}, f32[1024]{0:T(1024)S(1)}, u32[]{:S(2)}, u32[]{:S(2)}) collective-permute-start(f32[1024]{0:T(1024)S(1)} %fusion.2), channel_id=1, source_target_pairs={{0,6},{1,7},{2,0},{3,1},{4,2},{5,3},{6,4},{7,5},{8,14},{9,15},{10,... | collective-permute-start | bytes 12296 | tf_op jit(solution)/shard_map/ppermute | solution.py:180
  144.4 1.0 pad_maximum_fusion
  145.4 0.0 collective-permute-done.15
  145.4 0.0 collective-permute-done.16
  145.4 0.0 collective-permute-done.17
  145.4 0.6 add_multiply_fusion
  (22 shorter events, 0.1 us)
Async XLA Ops:
  5.4 25.8 %collective-permute-start.1 = (f32[512,512]{1,0:T(8,128)}, f32[512,512]{1,0:T(8,128)S(1)}, u32[]{:S(2)}, u32[]{:S(2)}) collective-permute-start(f32[512,512]{1,0:T(8,128)} %get-tuple-element.34), channel_id=1, source_target_pairs={{0,16},{8,24},{16,0},{24,8},{32,48},{40,56},{48,32},{56,40},{64,80... | collective-permute-start | bytes 3145736 | tf_op jit(solution)/shard_map/ppermute | solution.py:117
  9.1 27.4 %collective-permute-start = (f32[512,512]{1,0:T(8,128)}, f32[512,512]{1,0:T(8,128)S(1)}, u32[]{:S(2)}, u32[]{:S(2)}) collective-permute-start(f32[512,512]{1,0:T(8,128)} %get-tuple-element.30), channel_id=1, source_target_pairs={{0,224},{8,232},{16,240},{24,56},{32,0},{40,8},{48,16},{56,88},{64... | collective-permute-start | bytes 3145736 | tf_op jit(solution)/shard_map/ppermute | solution.py:117
  19.5 39.4 %collective-permute-start.5 = (f32[512,512]{1,0:T(8,128)}, f32[512,512]{1,0:T(8,128)S(1)}, u32[]{:S(2)}, u32[]{:S(2)}) collective-permute-start(f32[512,512]{1,0:T(8,128)} %get-tuple-element.38), channel_id=1, source_target_pairs={{0,224},{8,232},{16,48},{24,56},{32,0},{40,8},{48,80},{56,88},{64,... | collective-permute-start | bytes 3145736 | tf_op jit(solution)/shard_map/ppermute | solution.py:117
  31.3 1.0 copy-start.4
  37.9 22.6 %collective-permute-start.2 = (f32[512,512]{1,0:T(8,128)S(1)}, f32[512,512]{1,0:T(8,128)S(1)}, u32[]{:S(2)}, u32[]{:S(2)}) collective-permute-start(f32[512,512]{1,0:T(8,128)S(1)} %add.98), channel_id=1, source_target_pairs={{0,8},{8,16},{16,24},{24,0},{32,40},{40,48},{48,56},{56,32},{64,72... | collective-permute-start | bytes 3145736 | tf_op jit(solution)/shard_map/ppermute | solution.py:117
  38.3 20.7 %copy-start.1 = (f32[512,512]{1,0:T(8,128)S(1)}, f32[512,512]{1,0:T(8,128)}, u32[]{:S(2)}) copy-start(f32[512,512]{1,0:T(8,128)} %get-tuple-element.50) | copy-start | bytes 3145732
  38.3 28.4 %collective-permute-start.3 = (f32[512,512]{1,0:T(8,128)}, f32[512,512]{1,0:T(8,128)S(1)}, u32[]{:S(2)}, u32[]{:S(2)}) collective-permute-start(f32[512,512]{1,0:T(8,128)} %get-tuple-element.43), channel_id=1, source_target_pairs={{0,24},{8,0},{16,8},{24,16},{32,56},{40,32},{48,40},{56,48},{64,88... | collective-permute-start | bytes 3145736 | tf_op jit(solution)/shard_map/ppermute | solution.py:117
  49.9 15.0 %copy-start.9 = (f32[1024]{0:T(1024)S(1)}, f32[1024]{0:T(1024)}, u32[]{:S(2)}) copy-start(f32[1024]{0:T(1024)} %param.11) | copy-start | bytes 12292
  49.9 15.0 %copy-start.11 = (f32[1024]{0:T(1024)S(1)}, f32[1024]{0:T(1024)}, u32[]{:S(2)}) copy-start(f32[1024]{0:T(1024)} %param.9) | copy-start | bytes 12292
  49.9 15.0 %copy-start.10 = (f32[1024]{0:T(1024)S(1)}, f32[1024]{0:T(1024)}, u32[]{:S(2)}) copy-start(f32[1024]{0:T(1024)} %param.10) | copy-start | bytes 12292
  49.9 33.5 %copy-start = (f32[512,512]{1,0:T(8,128)S(1)}, f32[512,512]{1,0:T(8,128)}, u32[]{:S(2)}) copy-start(f32[512,512]{1,0:T(8,128)} %get-tuple-element.47) | copy-start | bytes 3145732
  60.5 1.0 copy-start.6
  61.6 21.8 %collective-permute-start.6 = (f32[512,512]{1,0:T(8,128)}, f32[512,512]{1,0:T(8,128)}, u32[]{:S(2)}, u32[]{:S(2)}) collective-permute-start(f32[512,512]{1,0:T(8,128)} %get-tuple-element.51), channel_id=1, source_target_pairs={{0,224},{8,232},{16,240},{24,56},{32,0},{40,8},{48,16},{56,88},{64... | collective-permute-start | bytes 3145736 | tf_op jit(solution)/shard_map/ppermute | solution.py:117
  64.9 20.0 %copy-start.5 = (f32[512,512]{1,0:T(8,128)S(1)}, f32[512,512]{1,0:T(8,128)}, u32[]{:S(2)}) copy-start(f32[512,512]{1,0:T(8,128)} %copy-done.4) | copy-start | bytes 3145732
  64.9 20.0 %copy-start.7 = (f32[512,512]{1,0:T(8,128)S(1)}, f32[512,512]{1,0:T(8,128)}, u32[]{:S(2)}) copy-start(f32[512,512]{1,0:T(8,128)} %copy-done.6) | copy-start | bytes 3145732
  64.9 20.0 %copy-start.8 = (f32[512,512]{1,0:T(8,128)S(1)}, f32[512,512]{1,0:T(8,128)}, u32[]{:S(2)}) copy-start(f32[512,512]{1,0:T(8,128)} %get-tuple-element.36) | copy-start | bytes 3145732
  64.9 36.6 %collective-permute-start.8 = (f32[512,512]{1,0:T(8,128)S(1)}, f32[512,512]{1,0:T(8,128)S(1)}, u32[]{:S(2)}, u32[]{:S(2)}) collective-permute-start(f32[512,512]{1,0:T(8,128)S(1)} %add.105), channel_id=1, source_target_pairs={{0,16},{8,24},{16,0},{24,8},{32,48},{40,56},{48,32},{56,40},{64,80... | collective-permute-start | bytes 3145736 | tf_op jit(solution)/shard_map/ppermute | solution.py:117
  66.7 31.4 %collective-permute-start.9 = (f32[256,512]{1,0:T(8,128)}, f32[256,512]{1,0:T(8,128)S(1)}, u32[]{:S(2)}, u32[]{:S(2)}) collective-permute-start(f32[256,512]{1,0:T(8,128)} %get-tuple-element.53), channel_id=1, source_target_pairs={{0,24},{8,0},{16,8},{24,16},{32,56},{40,32},{48,40},{56,48},{64,88... | collective-permute-start | bytes 1572872 | tf_op jit(solution)/shard_map/ppermute | solution.py:117
  84.8 15.4 %collective-permute-start.7 = (f32[256,512]{1,0:T(8,128)S(1)}, f32[256,512]{1,0:T(8,128)S(1)}, u32[]{:S(2)}, u32[]{:S(2)}) collective-permute-start(f32[256,512]{1,0:T(8,128)S(1)} %get-tuple-element.65), channel_id=1, source_target_pairs={{0,8},{8,16},{16,24},{24,0},{32,40},{40,48},{48,56},{56,32},{64,72... | collective-permute-start | bytes 1572872 | tf_op jit(solution)/shard_map/ppermute | solution.py:117
  84.9 15.3 %copy-start.12 = (f32[256,512]{1,0:T(8,128)S(1)}, f32[256,512]{1,0:T(8,128)}, u32[]{:S(2)}) copy-start(f32[256,512]{1,0:T(8,128)} %get-tuple-element.57) | copy-start | bytes 1572868
  84.9 16.5 %copy-start.2 = (f32[512,512]{1,0:T(8,128)S(1)}, f32[512,512]{1,0:T(8,128)}, u32[]{:S(2)}) copy-start(f32[512,512]{1,0:T(8,128)} %get-tuple-element.32) | copy-start | bytes 3145732
  86.9 14.6 %copy-start.3 = (f32[512,512]{1,0:T(8,128)S(1)}, f32[512,512]{1,0:T(8,128)}, u32[]{:S(2)}) copy-start(f32[512,512]{1,0:T(8,128)} %get-tuple-element.55) | copy-start | bytes 3145732
  86.9 24.8 %collective-permute-start.4 = (f32[512,512]{1,0:T(8,128)S(1)}, f32[512,512]{1,0:T(8,128)S(1)}, u32[]{:S(2)}, u32[]{:S(2)}) collective-permute-start(f32[512,512]{1,0:T(8,128)S(1)} %get-tuple-element.68), channel_id=1, source_target_pairs={{0,32},{8,40},{16,48},{24,56},{32,64},{40,72},{48,80},{56,88},{64,... | collective-permute-start | bytes 3145736 | tf_op jit(solution)/shard_map/ppermute | solution.py:117
  87.0 24.4 %collective-permute-start.11 = (f32[256,512]{1,0:T(8,128)S(1)}, f32[256,512]{1,0:T(8,128)S(1)}, u32[]{:S(2)}, u32[]{:S(2)}) collective-permute-start(f32[256,512]{1,0:T(8,128)S(1)} %get-tuple-element.64), channel_id=1, source_target_pairs={{0,8},{8,16},{16,24},{24,0},{32,40},{40,48},{48,56},{56,32},{64,72... | collective-permute-start | bytes 1572872 | tf_op jit(solution)/shard_map/ppermute | solution.py:117
  100.2 11.2 %collective-permute-start.12 = (f32[256,512]{1,0:T(8,128)S(1)}, f32[256,512]{1,0:T(8,128)S(1)}, u32[]{:S(2)}, u32[]{:S(2)}) collective-permute-start(f32[256,512]{1,0:T(8,128)S(1)} %copy-done.12), channel_id=1, source_target_pairs={{0,24},{8,0},{16,8},{24,16},{32,56},{40,32},{48,40},{56,48},{64,88... | collective-permute-start | bytes 1572872 | tf_op jit(solution)/shard_map/ppermute | solution.py:117
  101.8 18.2 %collective-permute-start.10 = (f32[256,512]{1,0:T(8,128)S(1)}, f32[256,512]{1,0:T(8,128)S(1)}, u32[]{:S(2)}, u32[]{:S(2)}) collective-permute-start(f32[256,512]{1,0:T(8,128)S(1)} %fusion.1), channel_id=1, source_target_pairs={{0,32},{8,40},{16,48},{24,56},{32,64},{40,72},{48,80},{56,88},{64,... | collective-permute-start | bytes 1572872 | tf_op jit(solution)/shard_map/ppermute | solution.py:117
  111.7 19.5 %collective-permute-start.13 = (f32[256,512]{1,0:T(8,128)S(1)}, f32[256,512]{1,0:T(8,128)S(1)}, u32[]{:S(2)}, u32[]{:S(2)}) collective-permute-start(f32[256,512]{1,0:T(8,128)S(1)} %fusion), channel_id=1, source_target_pairs={{0,32},{8,40},{16,48},{24,56},{32,64},{40,72},{48,80},{56,88},{64,... | collective-permute-start | bytes 1572872 | tf_op jit(solution)/shard_map/ppermute | solution.py:117
  132.0 6.7 %collective-permute-start.14 = (f32[1024]{0:T(1024)S(1)}, f32[1024]{0:T(1024)S(1)}, u32[]{:S(2)}, u32[]{:S(2)}) collective-permute-start(f32[1024]{0:T(1024)S(1)} %pad_maximum_fusion.1), channel_id=1, source_target_pairs={{0,1},{1,0},{2,3},{3,2},{4,5},{5,4},{6,7},{7,6},{8,9},{9,8},{10,11... | collective-permute-start | bytes 12296 | tf_op jit(solution)/shard_map/ppermute | solution.py:179
  138.8 6.7 %collective-permute-start.15 = (f32[1024]{0:T(1024)S(1)}, f32[1024]{0:T(1024)S(1)}, u32[]{:S(2)}, u32[]{:S(2)}) collective-permute-start(f32[1024]{0:T(1024)S(1)} %fusion.2), channel_id=1, source_target_pairs={{0,4},{1,5},{2,6},{3,7},{4,0},{5,1},{6,2},{7,3},{8,12},{9,13},{10,... | collective-permute-start | bytes 12296 | tf_op jit(solution)/shard_map/ppermute | solution.py:180
  141.7 3.7 %collective-permute-start.16 = (f32[1024]{0:T(1024)S(1)}, f32[1024]{0:T(1024)S(1)}, u32[]{:S(2)}, u32[]{:S(2)}) collective-permute-start(f32[1024]{0:T(1024)S(1)} %fusion.2), channel_id=1, source_target_pairs={{0,2},{1,3},{2,4},{3,5},{4,6},{5,7},{6,0},{7,1},{8,10},{9,11},{10,... | collective-permute-start | bytes 12296 | tf_op jit(solution)/shard_map/ppermute | solution.py:180
  142.1 3.3 %collective-permute-start.17 = (f32[1024]{0:T(1024)S(1)}, f32[1024]{0:T(1024)S(1)}, u32[]{:S(2)}, u32[]{:S(2)}) collective-permute-start(f32[1024]{0:T(1024)S(1)} %fusion.2), channel_id=1, source_target_pairs={{0,6},{1,7},{2,0},{3,1},{4,2},{5,3},{6,4},{7,5},{8,14},{9,15},{10,... | collective-permute-start | bytes 12296 | tf_op jit(solution)/shard_map/ppermute | solution.py:180
